TPU v7x, 512 devices: a whole 4x8x8 slice. The times are simulated.
512 devices in a mesh: prow: 16 (over z_lo, x, core), pcol: 32 (over z_hi, y).
Axes of the slice: x: 4, y: 8, z: 8 (z_hi: 4, z_lo: 2; z = z_hi * 2 + z_lo), core: 2. Of those that a mesh axis runs over, the one named last changes fastest.
Arguments:
- trailing: float32 [8192, 8192], P('prow', 'pcol'), may hold values from -6 to 6
- panels: float32 [8192, 1024], P('prow', 'pcol'), may hold values from -0.09375 to 0.09375
- diag_inv: float32 [4, 256, 256], replicated, may hold values from -6 to 6
- ancestors: int32 [4, 16], replicated, may hold values from 0 to 31, as said below
- owner_map: int32 [32], replicated, may hold values from 0 to 31, each once
Outputs:
- inv_panel: float32 [8192, 1024], P(('prow', 'pcol'))
- inv_upper: float32 [1024, 8192], P('pcol', 'prow')
- inv_diag: float32 [4, 256, 256], replicated
Inputs may be any that keep to these rules, and one draw needn't show every extreme that they name: `ancestors`: each row names 16 distinct blocks; every block is named by exactly two siblings.
All inputs are finite; a program needn't handle non-finite values.
Results may differ from a plain program's by a relative error of at most 0.000071.
Values sent between devices are 32-bit elements; how exact they have to be, the bound alone decides.
No kernel may reach another device: no remote copies, remote signals or barrier semaphores. Data moves between devices by JAX's collectives and lax.ppermute only.
A program may use at most 64 MiB of HBM per device.

v0:
```python
import jax
import jax.numpy as jnp
from jax import lax
from jax.sharding import PartitionSpec as P

NB = 256
SIBS = 4


def spread(array, axis, root):
    mine = lax.axis_index(axis) == root
    return lax.psum(jnp.where(mine, array, jnp.zeros_like(array)), axis)


def expand_cols(block_mask, ncols):
    siblings = jnp.arange(SIBS, dtype=jnp.int32)
    column_sib = jnp.arange(ncols, dtype=jnp.int32) // NB
    onehot = (column_sib[None, :] == siblings[:, None]).astype(jnp.float32)
    return jnp.dot(
        block_mask, onehot, precision=lax.Precision.HIGHEST, preferred_element_type=jnp.float32
    )


def shards(trailing, panels, diag_inv, ancestors, owner_map):
    row_index = lax.axis_index("prow")
    col_index = lax.axis_index("pcol")
    ncols_grid = lax.axis_size("pcol")
    nblk = owner_map.shape[0]
    rows_dev = trailing.shape[0]
    cols_dev = trailing.shape[1]
    row_blocks = rows_dev // NB
    col_blocks = cols_dev // NB
    part_rows = rows_dev // ncols_grid
    slots = owner_map[ancestors]
    member_t = (
        jnp.any(slots[:, :, None] == jnp.arange(nblk, dtype=jnp.int32)[None, None, :], axis=1)
        .astype(jnp.float32)
        .T
    )
    whole_rows = lax.all_gather(panels, "pcol", axis=1, tiled=True)
    mask_rows = lax.dynamic_slice_in_dim(member_t, row_index * row_blocks, row_blocks, 0)
    full_mask = jnp.repeat(expand_cols(mask_rows, whole_rows.shape[1]), NB, axis=0)
    masked_rows = whole_rows * full_mask
    first_col_block = col_index * col_blocks
    root = first_col_block // row_blocks
    offset = first_col_block % row_blocks * NB
    to_send = lax.dynamic_slice_in_dim(masked_rows, offset, cols_dev, 0)
    col_rows = spread(to_send, "prow", root)
    product = jnp.dot(
        trailing, col_rows, precision=lax.Precision.HIGHEST, preferred_element_type=jnp.float32
    )
    first_row = row_index * rows_dev + col_index * part_rows
    row_block = (first_row + jnp.arange(part_rows, dtype=jnp.int32)) // NB
    onehot_rows = (row_block[:, None] == jnp.arange(nblk, dtype=jnp.int32)[None, :]).astype(
        jnp.float32
    )
    row_member = jnp.dot(
        onehot_rows, member_t, precision=lax.Precision.HIGHEST, preferred_element_type=jnp.float32
    )
    reduced = lax.psum_scatter(product, "pcol", scatter_dimension=0, tiled=True)
    row_mask = jnp.repeat(row_member, NB, axis=1)
    inv_panel = -reduced * row_mask
    inv_upper = lax.all_to_all(inv_panel, "pcol", split_axis=1, concat_axis=0, tiled=True).T
    term = jnp.einsum(
        "rjn,rjm->jnm",
        masked_rows.reshape(rows_dev, SIBS, NB),
        product.reshape(rows_dev, SIBS, NB),
        precision=lax.Precision.HIGHEST,
    )
    inv_diag = diag_inv + lax.psum(term, ("prow", "pcol"))
    return (inv_panel, inv_upper, inv_diag)


def solution(mesh):
    placed = (P("prow", "pcol"), P("prow", "pcol"), P(), P(), P())
    return jax.shard_map(
        shards,
        mesh=mesh,
        in_specs=placed,
        out_specs=(P(("prow", "pcol"), None), P("pcol", "prow"), P()),
        check_vma=False,
    )
```

profile of v0, /device:TPU:1, one launch (start us, length us, event | category | flops | bytes accessed | tf_op | source)
XLA Modules:
  0.0 760.9 jit_solution(17372667747681556547)
XLA Ops:
  7.2 0.7 all-gather.2.cloned.1.call-update
  8.0 0.7 compare_select_fusion
  8.8 1.4 gather_fusion
  10.4 0.3 fusion.1
  10.7 1.2 broadcast_in_dim.9
  12.2 87.2 %all-gather.2.cloned.1.call-done = f32[512,1024]{0,1:T(8,128)} async-done(((f32[512,32]{0,1:T(8,128)}), f32[512,1024]{0,1:T(8,128)}) %all-gather.2.cloned.1.call-update) | async-done | bytes 2097168 | tf_op jit(solution)/shard_map/all_gather | solution.py:40
  99.4 2.1 mul.19
  101.5 1.3 copy-done.1
  102.8 1.1 dynamic-slice_select_fusion
  104.0 131.1 %all-reduce.3.cloned.1.call-done = f32[256,1024]{0,1:T(8,128)} async-done(((f32[256,1024]{0,1:T(8,128)}), f32[256,1024]{0,1:T(8,128)}) %all-reduce.3.cloned.1.call-update) | async-done | bytes 1048592 | tf_op jit(solution)/shard_map/psum | solution.py:12
  235.1 3.1 fusion.10
  238.2 1.8 copy.29
  240.0 4.6 fusion.11
  244.7 0.2 fusion.3
  244.9 221.9 %reduce-scatter.4.cloned.1.call-done = f32[16,1024]{1,0:T(8,128)} async-done(((f32[512,1024]{1,0:T(8,128)}), f32[16,1024]{1,0:T(8,128)}) %reduce-scatter.4.cloned.1.call-update) | async-done | bytes 65552
  466.9 1.0 copy.30
  468.1 0.8 reshape.70
  469.0 7.7 %all-to-all-start = ((f32[32,1,512]{2,1,0:T(1,128)}), f32[32,1,512]{2,1,0:T(1,128)S(1)}, u32[]{:S(2)}, u32[]{:S(2)}) async-start(f32[32,1,512]{2,1,0:T(1,128)} %reshape.70), calls=%async_computation | async-start | bytes 131072 | tf_op jit(solution)/shard_map/all_to_all | solution.py:63
  476.6 272.5 %all-reduce.5.cloned.1.call-done = f32[4,256,256]{2,1,0:T(8,128)} async-done(((f32[4,256,256]{2,1,0:T(8,128)}), f32[4,256,256]{2,1,0:T(8,128)}) %all-reduce.5.cloned.1.call-update) | async-done | bytes 1048592 | tf_op jit(solution)/shard_map/psum | solution.py:70
  749.1 2.3 add.57
  751.4 0.8 copy.25
  752.2 0.5 broadcast.78
  752.7 0.8 reduce
  753.7 0.7 copy.26
  (23 shorter events, 1.0 us)
Async XLA Ops:
  7.2 227.9 %copy-start = (f32[512,256]{1,0:T(8,128)S(1)}, f32[512,256]{1,0:T(8,128)}, u32[]{:S(2)}) copy-start(f32[512,256]{1,0:T(8,128)} %param.5) | copy-start | bytes 1572868
  7.2 92.2 %all-gather.2.cloned.1.call-start = ((), (), s32[]{:S(2)}) async-start(), calls=%async_computation.2 | async-start | bytes 2162688 | tf_op jit(solution)/shard_map/all_gather | solution.py:40
  7.9 227.2 %all-reduce.3.cloned.1.call-start = ((), (), s32[]{:S(2)}) async-start(), calls=%async_computation.3 | async-start | bytes 2097152 | tf_op jit(solution)/shard_map/psum | solution.py:12
  101.5 1.3 copy-start.1
  103.9 362.9 %reduce-scatter.4.cloned.1.call-start = ((), (), s32[]{:S(2)}) async-start(), calls=%async_computation.5 | async-start | bytes 2162688
  240.0 509.1 %all-reduce.5.cloned.1.call-start = ((), (), s32[]{:S(2)}) async-start(), calls=%async_computation.4 | async-start | bytes 2097152 | tf_op jit(solution)/shard_map/psum | solution.py:70
  244.7 504.4 %copy-start.2 = (f32[4,256,256]{2,1,0:T(8,128)S(1)}, f32[4,256,256]{2,1,0:T(8,128)}, u32[]{:S(2)}) copy-start(f32[4,256,256]{2,1,0:T(8,128)} %param.7) | copy-start | bytes 3145732
  469.0 283.3 %all-to-all-start = ((f32[32,1,512]{2,1,0:T(1,128)}), f32[32,1,512]{2,1,0:T(1,128)S(1)}, u32[]{:S(2)}, u32[]{:S(2)}) async-start(f32[32,1,512]{2,1,0:T(1,128)} %reshape.70), calls=%async_computation | async-start | bytes 131072 | tf_op jit(solution)/shard_map/all_to_all | solution.py:63
Sparse Core Ops, SparseCore 0:
  11.2 88.1 all-gather.1
  104.0 130.9 all-reduce.2
  240.1 226.7 reduce-scatter.3
  472.4 276.6 all-reduce.4
where the time goes:
time: 761 us
  waiting for transfers between devices  713 us (94%)
  between operations  13.9 us (2%)
  local copies, waits for them, and re-layouts  10.4 us (1%)
  matrix products  8.25 us (1%)
  starting transfers between devices  7.82 us (1%)
    psum x1, waiting for transfers between devices, shards(): inv_diag = diag_inv + lax.psum(term, ('prow', 'pcol'))  272 us
    unnamed x5, waiting for transfers between devices  223 us
    psum x1, waiting for transfers between devices, spread(): return lax.psum(jnp.where(mine, array, jnp.zeros_like(array)), axis)  131 us
    all_gather x1, waiting for transfers between devices, shards(): whole_rows = lax.all_gather(panels, 'pcol', axis=1, tiled=True)  87.2 us
  transfers between devices with their start and end apart: 5, of which 4 were waited for; matrix products, arithmetic and copies ran while one was open for 2% of the time, Pallas kernels for 0%

commit v1 on v0

v1 whole, which is shorter than its diff:
```python
import jax
import jax.numpy as jnp
import numpy as np
from jax import lax
from jax.sharding import Mesh, PartitionSpec as P

NB = 256
SIBS = 4
PROW = ("zlo", "x", "core")
PCOL = ("zhi", "y")
HIGH = lax.Precision.HIGH
HIGHEST = lax.Precision.HIGHEST


def exchange(array, axes):
    return lax.all_to_all(array, axes, 0, 0, tiled=True)


def pick(first, last, t):
    return first if t == 0 else last


def shards(trailing, panels, diag_inv, ancestors, owner_map):
    row = lax.axis_index(PROW)
    col = lax.axis_index(PCOL)
    nrow, ncol = 16, 32
    nblk = owner_map.shape[0]

    blocks = jnp.stack([col, 2 * row, 2 * row + 1, 2 * row + col // 16])
    number = jnp.sum(
        jnp.where(owner_map[None, :] == blocks[:, None], jnp.arange(nblk)[None, :], 0), axis=1
    )
    named = jnp.any(ancestors[None, :, :] == number[:, None, None], axis=2)
    sibling = jnp.arange(SIBS, dtype=jnp.int32)[None, :]
    first = jnp.min(jnp.where(named, sibling, SIBS), axis=1)
    last = jnp.max(jnp.where(named, sibling, -1), axis=1)

    factor_t = panels.T
    sib_rows = exchange(jnp.broadcast_to(factor_t[None], (8, 32, 512)), "y").reshape(256, 512)

    spread = exchange(factor_t.reshape(nrow, 2, 512), PROW)
    spread = spread.reshape(nrow, 2, 2, NB).transpose(0, 2, 1, 3).reshape(ncol, 2, NB)
    spread = exchange(spread, PCOL).reshape(SIBS, 16, NB)
    active = jnp.concatenate(
        [
            lax.dynamic_index_in_dim(spread, first[0], 0),
            lax.dynamic_index_in_dim(spread, last[0], 0),
        ],
        axis=0,
    )
    active = exchange(jnp.broadcast_to(active.reshape(1, 32, NB), (nrow, 32, NB)), PROW)
    active = active.reshape(nrow, 2, 16, NB)

    mine = (first[0], last[0])
    sides = []
    for h in range(2):
        for t in range(2):
            want = pick(first[1 + h], last[1 + h], t)
            sides.append(
                jnp.where(mine[0] == want, active[:, 0], 0.0)
                + jnp.where(mine[1] == want, active[:, 1], 0.0)
            )
    sides = jnp.stack(sides).reshape(2, 512, NB)
    product = lax.dot_general(
        trailing.reshape(2, NB, NB),
        sides,
        (((2,), (2,)), ((0,), (0,))),
        precision=HIGH,
        preferred_element_type=jnp.float32,
    )
    pieces = exchange(product.reshape(ncol, 16, 512), PCOL)
    reduced = jnp.sum(pieces, axis=0)

    source = jnp.arange(512, dtype=jnp.int32)
    slot = source // 256
    within = source % 16 // 2 * 32 + source % 256 // 16 * 2 + source % 2
    place = jnp.where(slot == 0, first[3], last[3]) * NB + within
    expand = jnp.where(place[:, None] == jnp.arange(1024, dtype=jnp.int32)[None, :], -1.0, 0.0)
    inv_panel = jnp.dot(reduced, expand, precision=HIGHEST, preferred_element_type=jnp.float32)

    upper = exchange(inv_panel.reshape(16, ncol, 32).transpose(1, 2, 0), PCOL)
    inv_upper = upper.transpose(1, 0, 2).reshape(32, 512)

    term = lax.dot_general(
        sib_rows,
        inv_upper,
        (((1,), (1,)), ((), ())),
        precision=HIGH,
        preferred_element_type=jnp.float32,
    )
    term = jnp.sum(exchange(term.reshape(nrow, 16, 32), PROW), axis=0)
    term = exchange(jnp.broadcast_to(term[None], (ncol, 16, 32)), PCOL)
    term = term.reshape(SIBS, 8, 16, 32).transpose(0, 2, 1, 3).reshape(64, NB)
    term = exchange(jnp.broadcast_to(term[None], (nrow, 64, NB)), PROW)
    term = term.reshape(nrow, SIBS, 16, NB).transpose(1, 0, 2, 3).reshape(SIBS, NB, NB)
    inv_diag = diag_inv - term
    return (inv_panel, inv_upper, inv_diag)


def solution(mesh):
    grid = Mesh(mesh.devices.reshape(2, 4, 2, 4, 8), PROW + PCOL)
    placed = (P(PROW, PCOL), P(PROW, PCOL), P(), P(), P())
    return jax.shard_map(
        shards,
        mesh=grid,
        in_specs=placed,
        out_specs=(P(PROW + PCOL, None), P(PCOL, PROW), P()),
        check_vma=False,
    )
```

time: 761 us -> 190 us (0.25)
  waiting for transfers between devices: 713 us -> 64.6 us
  blocking collectives: 0 us -> 50 us
  starting transfers between devices: 7.82 us -> 40.1 us
    psum x2 -> x0, waiting for transfers between devices: 404 us -> none  [the longest x1 272 us: shards(): inv_diag = diag_inv + lax.psum(term, ('prow', 'pcol'))]
    unnamed x5 -> x0, waiting for transfers between devices: 223 us -> none
    all_gather x1 -> x0, waiting for transfers between devices: 87.2 us -> none  [shards(): whole_rows = lax.all_gather(panels, 'pcol', axis=1, tiled=True)]
    all_to_all x1 -> x6, waiting for transfers between devices: 0.01 us -> 64.6 us  [exchange(): return lax.all_to_all(array, axes, 0, 0, tiled=True)]
    all_to_all x0 -> x3, blocking collectives: none -> 50 us  [exchange(): return lax.all_to_all(array, axes, 0, 0, tiled=True)]
    all_to_all x1 -> x6, starting transfers between devices: 7.66 us -> 40.1 us  [exchange(): return lax.all_to_all(array, axes, 0, 0, tiled=True)]
  transfers between devices with their start and end apart: 5 -> 6, of which waited for: 4 -> 5; matrix products, arithmetic and copies ran while one was open for 2% -> 3% of each run, Pallas kernels for 0% -> 0%
where the time goes in v1:
time: 190 us; the launch traced here: 189 us
  waiting for transfers between devices  64.6 us (34%)
  blocking collectives  50 us (26%)
  starting transfers between devices  40.1 us (21%)
  between operations  14.7 us (8%)
  local copies, waits for them, and re-layouts  9.62 us (5%)
  other arithmetic  6.96 us (4%)
  matrix products  3.26 us (2%)
    all_to_all x6, waiting for transfers between devices, exchange(): return lax.all_to_all(array, axes, 0, 0, tiled=True)  64.6 us
    all_to_all x3, blocking collectives, exchange(): return lax.all_to_all(array, axes, 0, 0, tiled=True)  50 us
    all_to_all x6, starting transfers between devices, exchange(): return lax.all_to_all(array, axes, 0, 0, tiled=True)  40.1 us
  transfers between devices with their start and end apart: 6, of which 5 were waited for; matrix products, arithmetic and copies ran while one was open for 3% of the time, Pallas kernels for 0%

profile of v1, /device:TPU:1, one launch (start us, length us, event | category | flops | bytes accessed | tf_op | source)
XLA Modules:
  0.0 189.3 jit_solution(11683994281096678292)
XLA Ops:
  0.6 1.6 reshape.250
  2.2 10.1 %all-to-all-start = ((f32[16,2,512]{2,1,0:T(2,128)}), f32[16,2,512]{2,1,0:T(2,128)S(1)}, u32[]{:S(2)}, u32[]{:S(2)}) async-start(f32[16,2,512]{2,1,0:T(2,128)} %reshape.250), calls=%async_computation | async-start | bytes 131072 | tf_op jit(solution)/shard_map/all_to_all | solution.py:16
  13.3 0.9 compare_reduce_fusion
  14.2 4.1 %all-to-all-done = f32[16,2,512]{2,1,0:T(2,128)S(1)} async-done(((f32[16,2,512]{2,1,0:T(2,128)}), f32[16,2,512]{2,1,0:T(2,128)S(1)}, u32[]{:S(2)}, u32[]{:S(2)}) %all-to-all-start) | async-done | bytes 65568 | tf_op jit(solution)/shard_map/all_to_all | solution.py:16
  19.0 12.2 %all-to-all-start.1 = ((f32[32,2,256]{2,1,0:T(2,128)}), f32[32,2,256]{2,1,0:T(2,128)S(1)}, u32[]{:S(2)}, u32[]{:S(2)}) async-start(f32[32,2,256]{2,1,0:T(2,128)} %reshape.251), calls=%async_computation.1 | async-start | bytes 131072 | tf_op jit(solution)/shard_map/all_to_all | solution.py:16
  35.8 6.6 %all-to-all-done.1 = f32[32,2,256]{2,1,0:T(2,128)S(1)} async-done(((f32[32,2,256]{2,1,0:T(2,128)}), f32[32,2,256]{2,1,0:T(2,128)S(1)}, u32[]{:S(2)}, u32[]{:S(2)}) %all-to-all-start.1) | async-done | bytes 65568 | tf_op jit(solution)/shard_map/all_to_all | solution.py:16
  42.5 0.8 broadcast_in_dim.100
  43.4 5.2 %all-to-all-start.2 = ((f32[16,32,256]{2,1,0:T(8,128)}), f32[16,32,256]{2,1,0:T(8,128)S(1)}, u32[]{:S(2)}, u32[]{:S(2)}) async-start(f32[16,32,256]{2,1,0:T(8,128)} %broadcast_in_dim.100), calls=%async_computation.2 | async-start | bytes 1048576 | tf_op jit(solution)/shard_map/all_to_all | solution.py:16
  58.9 1.6 fusion.45
  60.5 4.1 %all-to-all-start.3 = ((f32[32,16,512]{2,1,0:T(8,128)}), f32[32,16,512]{2,1,0:T(8,128)S(1)}, u32[]{:S(2)}, u32[]{:S(2)}) async-start(f32[32,16,512]{2,1,0:T(8,128)} %bitcast.25), calls=%async_computation.3 | async-start | bytes 2097152 | tf_op jit(solution)/shard_map/all_to_all | solution.py:16
  64.6 1.2 fusion.29
  65.8 25.7 %all-to-all-done.3 = f32[32,16,512]{2,1,0:T(8,128)S(1)} async-done(((f32[32,16,512]{2,1,0:T(8,128)}), f32[32,16,512]{2,1,0:T(8,128)S(1)}, u32[]{:S(2)}, u32[]{:S(2)}) %all-to-all-start.3) | async-done | bytes 1048608 | tf_op jit(solution)/shard_map/all_to_all | solution.py:16
  91.6 1.3 fusion
  93.4 20.6 %all_to_all.45 = f32[32,1,512]{2,1,0:T(1,128)S(1)} all-to-all(f32[32,1,512]{2,1,0:T(1,128)S(1)} %reshape.264), channel_id=1, replica_groups=mesh['zlo'=2,'x'=4,'core'=2,'zhi'=4,'y'=8] {'zhi','y'}, dimensions={0} | all-to-all | bytes 131072 | tf_op jit(solution)/shard_map/all_to_all | solution.py:16
  114.0 0.9 broadcast_in_dim.106
  114.8 3.5 %all-to-all-start.5 = ((f32[8,32,512]{2,1,0:T(8,128)}), f32[8,32,512]{2,1,0:T(8,128)S(1)}, u32[]{:S(2)}, u32[]{:S(2)}) async-start(f32[8,32,512]{2,1,0:T(8,128)} %broadcast_in_dim.106), calls=%async_computation.5 | async-start | bytes 1048576 | tf_op jit(solution)/shard_map/all_to_all | solution.py:16
  119.8 13.2 %all-to-all-done.5 = f32[8,32,512]{2,1,0:T(8,128)S(1)} async-done(((f32[8,32,512]{2,1,0:T(8,128)}), f32[8,32,512]{2,1,0:T(8,128)S(1)}, u32[]{:S(2)}, u32[]{:S(2)}) %all-to-all-start.5) | async-done | bytes 524320 | tf_op jit(solution)/shard_map/all_to_all | solution.py:16
  133.5 15.2 %all_to_all.46 = f32[16,1,512]{2,1,0:T(1,128)S(1)} all-to-all(f32[16,1,512]{2,1,0:T(1,128)S(1)} %reshape.266), channel_id=1, replica_groups=mesh['zlo'=2,'x'=4,'core'=2,'zhi'=4,'y'=8] {'zlo','x','core'}, dimensions={0} | all-to-all | bytes 65536 | tf_op jit(solution)/shard_map/all_to_all | solution.py:16
  149.7 14.2 %all_to_all.47 = f32[32,1,512]{2,1,0:T(1,128)S(1)} all-to-all(f32[32,1,512]{2,1,0:T(1,128)S(1)} %reshape.268), channel_id=1, replica_groups=mesh['zlo'=2,'x'=4,'core'=2,'zhi'=4,'y'=8] {'zhi','y'}, dimensions={0} | all-to-all | bytes 131072 | tf_op jit(solution)/shard_map/all_to_all | solution.py:16
  165.1 1.1 broadcast_in_dim.109
  166.2 5.0 %all-to-all-start.8 = ((f32[16,64,256]{2,1,0:T(8,128)}), f32[16,64,256]{2,1,0:T(8,128)S(1)}, u32[]{:S(2)}, u32[]{:S(2)}) async-start(f32[16,64,256]{2,1,0:T(8,128)} %broadcast_in_dim.109), calls=%async_computation.8 | async-start | bytes 2097152 | tf_op jit(solution)/shard_map/all_to_all | solution.py:16
  171.9 15.0 %all-to-all-done.8 = f32[16,64,256]{2,1,0:T(8,128)S(1)} async-done(((f32[16,64,256]{2,1,0:T(8,128)}), f32[16,64,256]{2,1,0:T(8,128)S(1)}, u32[]{:S(2)}, u32[]{:S(2)}) %all-to-all-start.8) | async-done | bytes 1048608 | tf_op jit(solution)/shard_map/all_to_all | solution.py:16
  187.0 1.1 copy-done.1
  188.2 1.1 bitcast_subtract_fusion
  (42 shorter events, 8.2 us)
Async XLA Ops:
  0.6 58.3 %copy-start = (f32[512,256]{1,0:T(8,128)S(1)}, f32[512,256]{1,0:T(8,128)}, u32[]{:S(2)}) copy-start(f32[512,256]{1,0:T(8,128)} %param.5) | copy-start | bytes 1572868
  2.2 16.0 %all-to-all-start = ((f32[16,2,512]{2,1,0:T(2,128)}), f32[16,2,512]{2,1,0:T(2,128)S(1)}, u32[]{:S(2)}, u32[]{:S(2)}) async-start(f32[16,2,512]{2,1,0:T(2,128)} %reshape.250), calls=%async_computation | async-start | bytes 131072 | tf_op jit(solution)/shard_map/all_to_all | solution.py:16
  19.0 23.5 %all-to-all-start.1 = ((f32[32,2,256]{2,1,0:T(2,128)}), f32[32,2,256]{2,1,0:T(2,128)S(1)}, u32[]{:S(2)}, u32[]{:S(2)}) async-start(f32[32,2,256]{2,1,0:T(2,128)} %reshape.251), calls=%async_computation.1 | async-start | bytes 131072 | tf_op jit(solution)/shard_map/all_to_all | solution.py:16
  43.4 15.2 %all-to-all-start.2 = ((f32[16,32,256]{2,1,0:T(8,128)}), f32[16,32,256]{2,1,0:T(8,128)S(1)}, u32[]{:S(2)}, u32[]{:S(2)}) async-start(f32[16,32,256]{2,1,0:T(8,128)} %broadcast_in_dim.100), calls=%async_computation.2 | async-start | bytes 1048576 | tf_op jit(solution)/shard_map/all_to_all | solution.py:16
  60.5 31.0 %all-to-all-start.3 = ((f32[32,16,512]{2,1,0:T(8,128)}), f32[32,16,512]{2,1,0:T(8,128)S(1)}, u32[]{:S(2)}, u32[]{:S(2)}) async-start(f32[32,16,512]{2,1,0:T(8,128)} %bitcast.25), calls=%async_computation.3 | async-start | bytes 2097152 | tf_op jit(solution)/shard_map/all_to_all | solution.py:16
  91.6 22.4 %copy-start.2 = (f32[512,32]{0,1:T(8,128)S(1)}, f32[512,32]{0,1:T(8,128)}, u32[]{:S(2)}) copy-start(f32[512,32]{0,1:T(8,128)} %param.6) | copy-start | bytes 196612
  92.9 21.9 %copy-start.3 = (f32[16,1024]{1,0:T(8,128)}, f32[16,1024]{1,0:T(8,128)S(1)}, u32[]{:S(2)}) copy-start(f32[16,1024]{1,0:T(8,128)S(1)} %fusion) | copy-start | bytes 196612
  114.8 18.1 %all-to-all-start.5 = ((f32[8,32,512]{2,1,0:T(8,128)}), f32[8,32,512]{2,1,0:T(8,128)S(1)}, u32[]{:S(2)}, u32[]{:S(2)}) async-start(f32[8,32,512]{2,1,0:T(8,128)} %broadcast_in_dim.106), calls=%async_computation.5 | async-start | bytes 1048576 | tf_op jit(solution)/shard_map/all_to_all | solution.py:16
  166.2 20.7 %all-to-all-start.8 = ((f32[16,64,256]{2,1,0:T(8,128)}), f32[16,64,256]{2,1,0:T(8,128)S(1)}, u32[]{:S(2)}, u32[]{:S(2)}) async-start(f32[16,64,256]{2,1,0:T(8,128)} %broadcast_in_dim.109), calls=%async_computation.8 | async-start | bytes 2097152 | tf_op jit(solution)/shard_map/all_to_all | solution.py:16
  186.9 1.2 copy-start.1

commit v2 on v1

v2 whole, which is shorter than its diff:
```python
import jax
import jax.numpy as jnp
from jax import lax
from jax.sharding import Mesh, PartitionSpec as P

NB = 256
SIBS = 4
PROW = ("zlo", "x", "core")
PCOL = ("zhi", "yhi", "ylo")
NROW = 16
NCOL = 32
HIGH = lax.Precision.HIGH


def exchange(array, axes):
    return lax.all_to_all(array, axes, 0, 0, tiled=True)


def to_all(array, count):
    return jnp.broadcast_to(array[None], (count,) + array.shape)


def column_of_block():
    pairs = []
    for p in range(NROW):
        for s in range(SIBS):
            for c in range(8):
                source = p * NCOL + s * 8 + c
                target = (c * 2 + s // 2) * NCOL + 2 * p + s % 2
                pairs.append((source, target))
    return pairs


def shards(trailing, panels, diag_inv, ancestors, owner_map):
    row = lax.axis_index(PROW)
    col = lax.axis_index(PCOL)
    core = lax.axis_index("core")
    nblk = owner_map.shape[0]

    factor_t = panels.T
    moved = lax.ppermute(factor_t, PROW + PCOL, column_of_block())

    blocks = jnp.stack([col, 2 * row, 2 * row + 1, 2 * row + col // 16])
    number = jnp.sum(
        jnp.where(owner_map[None, :] == blocks[:, None], jnp.arange(nblk)[None, :], 0), axis=1
    )
    named = jnp.any(ancestors[None, :, :] == number[:, None, None], axis=2)
    sibling = jnp.arange(SIBS, dtype=jnp.int32)[None, :]
    first = jnp.min(jnp.where(named, sibling, SIBS), axis=1)
    last = jnp.max(jnp.where(named, sibling, -1), axis=1)

    halves = moved.reshape(32, 2, NB).transpose(1, 0, 2)
    whole = exchange(to_all(halves, NROW).reshape(NCOL, 32, NB), PROW + ("ylo",))
    whole = whole.reshape(8, SIBS, 32, NB)

    sides = []
    for h in range(2):
        for want in (first[1 + h], last[1 + h]):
            side = lax.dynamic_index_in_dim(whole, want, 1)
            held = (first[0] == want) | (last[0] == want)
            sides.append(jnp.where(held, side, 0.0))
    sides = jnp.stack(sides).reshape(2, 512, NB)
    product = lax.dot_general(
        trailing.reshape(2, NB, NB),
        sides,
        (((2,), (2,)), ((0,), (0,))),
        precision=HIGH,
        preferred_element_type=jnp.float32,
    )
    pieces = exchange(product.reshape(NCOL, 16, 512), PCOL)
    reduced = jnp.sum(pieces, axis=0).reshape(16, 2, NB)

    result = jnp.stack(
        [
            jnp.where(
                first[3] == s, -reduced[:, 0], jnp.where(last[3] == s, -reduced[:, 1], 0.0)
            )
            for s in range(SIBS)
        ]
    )
    inv_panel = result.transpose(1, 0, 2).reshape(16, SIBS * NB)

    upper = jnp.broadcast_to(result[:, None], (SIBS, 8, 16, NB)).reshape(NCOL, 16, NB)
    upper = exchange(upper, PCOL).reshape(512, NB)
    part = lax.dynamic_slice_in_dim(upper, col % 8 * 32, 32, 1)
    inv_upper = part.T

    term = jnp.dot(factor_t, upper, precision=HIGH, preferred_element_type=jnp.float32)
    term = exchange(to_all(term.reshape(2, 16, NB), 8).reshape(NROW, 16, NB), PROW)
    term = jnp.sum(term, axis=0)
    mine = exchange(to_all(term, NCOL), PCOL)
    other = lax.ppermute(mine, "core", [(0, 1), (1, 0)])
    low = jnp.where(core == 0, mine, other).reshape(SIBS, 8, 1, 16, NB)
    high = jnp.where(core == 0, other, mine).reshape(SIBS, 8, 1, 16, NB)
    term = jnp.concatenate([low, high], axis=2).reshape(SIBS, NB, NB)
    inv_diag = diag_inv - term
    return (inv_panel, inv_upper, inv_diag)


def solution(mesh):
    grid = Mesh(mesh.devices.reshape(2, 4, 2, 4, 4, 2), PROW + PCOL)
    placed = (P(PROW, PCOL), P(PROW, PCOL), P(), P(), P())
    return jax.shard_map(
        shards,
        mesh=grid,
        in_specs=placed,
        out_specs=(P(PROW + PCOL, None), P(PCOL, PROW), P()),
        check_vma=False,
    )
```

time: 190 us -> 164 us (0.86)
  waiting for transfers between devices: 64.6 us -> 30.5 us
  blocking collectives: 50 us -> 63.4 us
  between operations: 14.7 us -> 23.6 us
  other arithmetic: 6.96 us -> 2.32 us
  local copies, waits for them, and re-layouts: 9.62 us -> 5.22 us
  starting transfers between devices: 40.1 us -> 35.8 us
    all_to_all x6 -> x2, waiting for transfers between devices: 64.6 us -> 21.9 us  [exchange(): return lax.all_to_all(array, axes, 0, 0, tiled=True)]
    all_to_all x6 -> x2, starting transfers between devices: 40.1 us -> 24.4 us  [exchange(): return lax.all_to_all(array, axes, 0, 0, tiled=True)]
    all_to_all x3, blocking collectives: 50 us -> 63.4 us  [exchange(): return lax.all_to_all(array, axes, 0, 0, tiled=True)]
    ppermute x0 -> x2, starting transfers between devices: none -> 11.4 us  [the longest x1 5.73 us: shards(): moved = lax.ppermute(factor_t, PROW + PCOL, column_of_block())]
    ppermute x0 -> x2, waiting for transfers between devices: none -> 8.57 us  [the longest x1 8.56 us: shards(): moved = lax.ppermute(factor_t, PROW + PCOL, column_of_block())]
    reshape x5 -> x2, local copies, waits for them, and re-layouts: 2.57 us -> 0.07 us  [the longest x1 0.04 us: shards(): halves = moved.reshape(32, 2, NB).transpose(1, 0, 2)]
    all_to_all x3 -> x0, other arithmetic: 2.32 us -> none  [exchange(): return lax.all_to_all(array, axes, 0, 0, tiled=True)]
  transfers between devices with their start and end apart: 6 -> 4, of which waited for: 5 -> 2; matrix products, arithmetic and copies ran while one was open for 3% -> 2% of each run, Pallas kernels for 0% -> 0%
where the time goes in v2:
time: 164 us; the launch traced here: 163 us
  blocking collectives  63.4 us (39%)
  starting transfers between devices  35.8 us (22%)
  waiting for transfers between devices  30.5 us (19%)
  between operations  23.6 us (14%)
  local copies, waits for them, and re-layouts  5.22 us (3%)
  other arithmetic  2.32 us (1%)
  matrix products  1.84 us (1%)
    all_to_all x3, blocking collectives, exchange(): return lax.all_to_all(array, axes, 0, 0, tiled=True)  63.4 us
    all_to_all x2, starting transfers between devices, exchange(): return lax.all_to_all(array, axes, 0, 0, tiled=True)  24.4 us
    all_to_all x2, waiting for transfers between devices, exchange(): return lax.all_to_all(array, axes, 0, 0, tiled=True)  21.9 us
    ppermute x1, waiting for transfers between devices, shards(): moved = lax.ppermute(factor_t, PROW + PCOL, column_of_block())  8.56 us
    ppermute x1, starting transfers between devices, shards(): moved = lax.ppermute(factor_t, PROW + PCOL, column_of_block())  5.73 us
    ppermute x1, starting transfers between devices, shards(): other = lax.ppermute(mine, 'core', [(0, 1), (1, 0)])  5.7 us
  transfers between devices with their start and end apart: 4, of which 2 were waited for; matrix products, arithmetic and copies ran while one was open for 2% of the time, Pallas kernels for 0%

profile of v2, /device:TPU:1, one launch (start us, length us, event | category | flops | bytes accessed | tf_op | source)
XLA Modules:
  0.0 162.6 jit_solution(17672819533356299289)
XLA Ops:
  0.6 5.7 %collective-permute-start = (f32[32,512]{1,0:T(8,128)}, f32[32,512]{1,0:T(8,128)S(1)}, u32[]{:S(2)}, u32[]{:S(2)}) collective-permute-start(f32[32,512]{1,0:T(8,128)} %bitcast.91), channel_id=1, source_target_pairs={{0,0},{1,64},{2,128},{3,192},{4,256},{5,320},{6,384},{7,448},{8,1}... | collective-permute-start | bytes 196616 | tf_op jit(solution)/shard_map/ppermute | solution.py:41
  6.4 8.6 %collective-permute-done = f32[32,512]{1,0:T(8,128)S(1)} collective-permute-done((f32[32,512]{1,0:T(8,128)}, f32[32,512]{1,0:T(8,128)S(1)}, u32[]{:S(2)}, u32[]{:S(2)}) %collective-permute-start) | collective-permute-done | bytes 65568 | tf_op jit(solution)/shard_map/ppermute | solution.py:41
  15.0 1.1 broadcast_in_dim.83
  16.1 12.2 %all-to-all-start = ((f32[32,32,256]{2,1,0:T(8,128)}), f32[32,32,256]{2,1,0:T(8,128)S(1)}, u32[]{:S(2)}, u32[]{:S(2)}) async-start(f32[32,32,256]{2,1,0:T(8,128)} %bitcast.10), calls=%async_computation | async-start | bytes 2097152 | tf_op jit(solution)/shard_map/all_to_all | solution.py:16
  28.4 0.1 pad_add_fusion
  28.4 0.6 copy-done.4
  29.0 0.2 select_reduce_fusion.2
  29.2 0.2 compare_reduce_fusion
  29.4 0.2 select_reduce_fusion
  29.6 0.7 fusion.8
  48.1 1.6 fusion.10
  49.7 12.2 %all-to-all-start.1 = ((f32[32,16,512]{2,1,0:T(8,128)}), f32[32,16,512]{2,1,0:T(8,128)S(1)}, u32[]{:S(2)}, u32[]{:S(2)}) async-start(f32[32,16,512]{2,1,0:T(8,128)} %bitcast.23), calls=%async_computation.1 | async-start | bytes 2097152 | tf_op jit(solution)/shard_map/all_to_all | solution.py:16
  66.9 21.9 %all-to-all-done.1 = f32[32,16,512]{2,1,0:T(8,128)S(1)} async-done(((f32[32,16,512]{2,1,0:T(8,128)}), f32[32,16,512]{2,1,0:T(8,128)S(1)}, u32[]{:S(2)}, u32[]{:S(2)}) %all-to-all-start.1) | async-done | bytes 1048608 | tf_op jit(solution)/shard_map/all_to_all | solution.py:16
  89.2 27.1 %all_to_all.25 = f32[32,16,256]{2,1,0:T(8,128)S(1)} all-to-all(f32[32,16,256]{2,1,0:T(8,128)S(1)} %bitcast.86), channel_id=1, replica_groups=mesh['zlo'=2,'x'=4,'core'=2,'zhi'=4,'yhi'=4,'ylo'=2] {'zhi','yhi','ylo'}, dimensions={0} | all-to-all | bytes 1048576 | tf_op jit(solution)/shard_map/all_to_all | solution.py:16
  116.3 0.3 fusion.11
  116.6 15.0 %all_to_all.26 = f32[16,16,256]{2,1,0:T(8,128)S(1)} all-to-all(f32[16,16,256]{2,1,0:T(8,128)S(1)} %bitcast.87), channel_id=1, replica_groups=mesh['zlo'=2,'x'=4,'core'=2,'zhi'=4,'yhi'=4,'ylo'=2] {'zlo','x','core'}, dimensions={0} | all-to-all | bytes 524288 | tf_op jit(solution)/shard_map/all_to_all | solution.py:16
  131.7 21.3 %all_to_all.27 = f32[32,16,256]{2,1,0:T(8,128)S(1)} all-to-all(f32[32,16,256]{2,1,0:T(8,128)S(1)} %broadcast_in_dim.89), channel_id=1, replica_groups=mesh['zlo'=2,'x'=4,'core'=2,'zhi'=4,'yhi'=4,'ylo'=2] {'zhi','yhi','ylo'}, dimensions={0} | all-to-all | bytes 1048576 | tf_op jit(solution)/shard_map/all_to_all | solution.py:16
  152.9 5.7 %collective-permute-start.1 = (f32[32,16,256]{2,1,0:T(8,128)S(1)}, f32[32,16,256]{2,1,0:T(8,128)S(1)}, u32[]{:S(2)}, u32[]{:S(2)}) collective-permute-start(f32[32,16,256]{2,1,0:T(8,128)S(1)} %all_to_all.27), channel_id=1, source_target_pairs={{0,32},{32,0},{1,33},{33,1},{2,34},{34,2},{3,35},{35,3},{4,36},{36... | collective-permute-start | bytes 1572872 | tf_op jit(solution)/shard_map/ppermute | solution.py:92
  158.7 0.6 copy.30
  159.3 0.1 dynamic-slice_bitcast_fusion
  159.4 0.7 copy.26
  160.2 0.1 broadcast_select_fusion.1
  160.4 1.1 copy-done.1
  161.5 1.1 bitcast_subtract_fusion
  (25 shorter events, 0.7 us)
Async XLA Ops:
  0.6 47.5 %copy-start = (f32[512,256]{1,0:T(8,128)S(1)}, f32[512,256]{1,0:T(8,128)}, u32[]{:S(2)}) copy-start(f32[512,256]{1,0:T(8,128)} %param.5) | copy-start | bytes 1572868
  0.6 14.3 %collective-permute-start = (f32[32,512]{1,0:T(8,128)}, f32[32,512]{1,0:T(8,128)S(1)}, u32[]{:S(2)}, u32[]{:S(2)}) collective-permute-start(f32[32,512]{1,0:T(8,128)} %bitcast.91), channel_id=1, source_target_pairs={{0,0},{1,64},{2,128},{3,192},{4,256},{5,320},{6,384},{7,448},{8,1}... | collective-permute-start | bytes 196616 | tf_op jit(solution)/shard_map/ppermute | solution.py:41
  16.1 31.8 %all-to-all-start = ((f32[32,32,256]{2,1,0:T(8,128)}), f32[32,32,256]{2,1,0:T(8,128)S(1)}, u32[]{:S(2)}, u32[]{:S(2)}) async-start(f32[32,32,256]{2,1,0:T(8,128)} %bitcast.10), calls=%async_computation | async-start | bytes 2097152 | tf_op jit(solution)/shard_map/all_to_all | solution.py:16
  28.3 0.7 copy-start.4
  28.4 0.8 copy-start.3
  49.7 39.1 %all-to-all-start.1 = ((f32[32,16,512]{2,1,0:T(8,128)}), f32[32,16,512]{2,1,0:T(8,128)S(1)}, u32[]{:S(2)}, u32[]{:S(2)}) async-start(f32[32,16,512]{2,1,0:T(8,128)} %bitcast.23), calls=%async_computation.1 | async-start | bytes 2097152 | tf_op jit(solution)/shard_map/all_to_all | solution.py:16
  89.1 27.1 %copy-start.2 = (f32[512,32]{0,1:T(8,128)S(1)}, f32[512,32]{0,1:T(8,128)}, u32[]{:S(2)}) copy-start(f32[512,32]{0,1:T(8,128)} %param.6) | copy-start | bytes 196612
  152.9 7.3 %collective-permute-start.1 = (f32[32,16,256]{2,1,0:T(8,128)S(1)}, f32[32,16,256]{2,1,0:T(8,128)S(1)}, u32[]{:S(2)}, u32[]{:S(2)}) collective-permute-start(f32[32,16,256]{2,1,0:T(8,128)S(1)} %all_to_all.27), channel_id=1, source_target_pairs={{0,32},{32,0},{1,33},{33,1},{2,34},{34,2},{3,35},{35,3},{4,36},{36... | collective-permute-start | bytes 1572872 | tf_op jit(solution)/shard_map/ppermute | solution.py:92
  160.3 1.2 copy-start.1

commit v3 on v2

--- a/solution.py
+++ b/solution.py
@@ -49,16 +49,23 @@
     first = jnp.min(jnp.where(named, sibling, SIBS), axis=1)
     last = jnp.max(jnp.where(named, sibling, -1), axis=1)
 
-    halves = moved.reshape(32, 2, NB).transpose(1, 0, 2)
-    whole = exchange(to_all(halves, NROW).reshape(NCOL, 32, NB), PROW + ("ylo",))
-    whole = whole.reshape(8, SIBS, 32, NB)
+    parts = moved.reshape(2, 16, 2, NB).transpose(0, 2, 1, 3).reshape(SIBS, 16, NB)
+    parts = exchange(parts, ("core", "ylo"))
+    parts = jnp.concatenate(
+        [
+            lax.dynamic_index_in_dim(parts, first[0], 0),
+            lax.dynamic_index_in_dim(parts, last[0], 0),
+        ]
+    )
+    block = exchange(to_all(parts.reshape(32, NB), NROW), PROW).reshape(NROW, 2, 16, NB)
 
     sides = []
     for h in range(2):
         for want in (first[1 + h], last[1 + h]):
-            side = lax.dynamic_index_in_dim(whole, want, 1)
-            held = (first[0] == want) | (last[0] == want)
-            sides.append(jnp.where(held, side, 0.0))
+            sides.append(
+                jnp.where(first[0] == want, block[:, 0], 0.0)
+                + jnp.where(last[0] == want, block[:, 1], 0.0)
+            )
     sides = jnp.stack(sides).reshape(2, 512, NB)
     product = lax.dot_general(
         trailing.reshape(2, NB, NB),

time: 164 us -> 163 us (level)
  between operations: 23.6 us -> 19.2 us
  starting transfers between devices: 35.8 us -> 39.3 us
    all_to_all x2 -> x3, starting transfers between devices: 24.4 us -> 27.9 us  [exchange(): return lax.all_to_all(array, axes, 0, 0, tiled=True)]
    all_to_all x2 -> x3, waiting for transfers between devices: 21.9 us -> 22 us  [exchange(): return lax.all_to_all(array, axes, 0, 0, tiled=True)]
  transfers between devices with their start and end apart: 4 -> 5, of which waited for: 2 -> 2; matrix products, arithmetic and copies ran while one was open for 2% -> 2% of each run, Pallas kernels for 0% -> 0%
where the time goes in v3:
time: 163 us; the launch traced here: 161 us
  blocking collectives  63.4 us (39%)
  starting transfers between devices  39.3 us (24%)
  waiting for transfers between devices  29.3 us (18%)
  between operations  19.2 us (12%)
  local copies, waits for them, and re-layouts  5.6 us (3%)
  other arithmetic  2.38 us (1%)
  matrix products  1.85 us (1%)
    all_to_all x3, blocking collectives, exchange(): return lax.all_to_all(array, axes, 0, 0, tiled=True)  63.4 us
    all_to_all x3, starting transfers between devices, exchange(): return lax.all_to_all(array, axes, 0, 0, tiled=True)  27.9 us
    all_to_all x3, waiting for transfers between devices, exchange(): return lax.all_to_all(array, axes, 0, 0, tiled=True)  22 us
    ppermute x1, waiting for transfers between devices, shards(): moved = lax.ppermute(factor_t, PROW + PCOL, column_of_block())  7.32 us
    ppermute x1, starting transfers between devices, shards(): moved = lax.ppermute(factor_t, PROW + PCOL, column_of_block())  5.73 us
    ppermute x1, starting transfers between devices, shards(): other = lax.ppermute(mine, 'core', [(0, 1), (1, 0)])  5.7 us
  transfers between devices with their start and end apart: 5, of which 2 were waited for; matrix products, arithmetic and copies ran while one was open for 2% of the time, Pallas kernels for 0%

profile of v3, /device:TPU:1, one launch (start us, length us, event | category | flops | bytes accessed | tf_op | source)
XLA Modules:
  0.0 161.1 jit_solution(598122052523977562)
XLA Ops:
  0.6 5.7 %collective-permute-start = (f32[32,512]{1,0:T(8,128)}, f32[32,512]{1,0:T(8,128)S(1)}, u32[]{:S(2)}, u32[]{:S(2)}) collective-permute-start(f32[32,512]{1,0:T(8,128)} %bitcast.113), channel_id=1, source_target_pairs={{0,0},{1,64},{2,128},{3,192},{4,256},{5,320},{6,384},{7,448},{8,1}... | collective-permute-start | bytes 196616 | tf_op jit(solution)/shard_map/ppermute | solution.py:41
  6.5 0.6 copy-done.4
  7.1 0.2 select_reduce_fusion.2
  7.3 0.2 compare_reduce_fusion
  7.5 0.2 select_reduce_fusion
  7.6 7.3 %collective-permute-done = f32[32,512]{1,0:T(8,128)S(1)} collective-permute-done((f32[32,512]{1,0:T(8,128)}, f32[32,512]{1,0:T(8,128)S(1)}, u32[]{:S(2)}, u32[]{:S(2)}) %collective-permute-start) | collective-permute-done | bytes 65568 | tf_op jit(solution)/shard_map/ppermute | solution.py:41
  15.0 0.6 copy.26
  15.6 3.3 %all-to-all-start = ((f32[4,16,256]{2,1,0:T(8,128)}), f32[4,16,256]{2,1,0:T(8,128)S(1)}, u32[]{:S(2)}, u32[]{:S(2)}) async-start(f32[4,16,256]{2,1,0:T(8,128)} %bitcast.9), calls=%async_computation | async-start | bytes 131072 | tf_op jit(solution)/shard_map/all_to_all | solution.py:16
  18.9 0.7 fusion.12
  23.2 0.8 broadcast_in_dim.89
  24.0 10.7 %all-to-all-start.1 = ((f32[16,32,256]{2,1,0:T(8,128)}), f32[16,32,256]{2,1,0:T(8,128)S(1)}, u32[]{:S(2)}, u32[]{:S(2)}) async-start(f32[16,32,256]{2,1,0:T(8,128)} %broadcast_in_dim.89), calls=%async_computation.1 | async-start | bytes 1048576 | tf_op jit(solution)/shard_map/all_to_all | solution.py:16
  44.7 1.6 fusion.14
  46.3 13.9 %all-to-all-start.2 = ((f32[32,16,512]{2,1,0:T(8,128)}), f32[32,16,512]{2,1,0:T(8,128)S(1)}, u32[]{:S(2)}, u32[]{:S(2)}) async-start(f32[32,16,512]{2,1,0:T(8,128)} %bitcast.28), calls=%async_computation.2 | async-start | bytes 2097152 | tf_op jit(solution)/shard_map/all_to_all | solution.py:16
  65.3 22.0 %all-to-all-done.2 = f32[32,16,512]{2,1,0:T(8,128)S(1)} async-done(((f32[32,16,512]{2,1,0:T(8,128)}), f32[32,16,512]{2,1,0:T(8,128)S(1)}, u32[]{:S(2)}, u32[]{:S(2)}) %all-to-all-start.2) | async-done | bytes 1048608 | tf_op jit(solution)/shard_map/all_to_all | solution.py:16
  87.6 24.9 %all_to_all.30 = f32[32,16,256]{2,1,0:T(8,128)S(1)} all-to-all(f32[32,16,256]{2,1,0:T(8,128)S(1)} %bitcast.107), channel_id=1, replica_groups=mesh['zlo'=2,'x'=4,'core'=2,'zhi'=4,'yhi'=4,'ylo'=2] {'zhi','yhi','ylo'}, dimensions={0} | all-to-all | bytes 1048576 | tf_op jit(solution)/shard_map/all_to_all | solution.py:16
  112.5 0.3 fusion.15
  112.8 17.3 %all_to_all.31 = f32[16,16,256]{2,1,0:T(8,128)S(1)} all-to-all(f32[16,16,256]{2,1,0:T(8,128)S(1)} %bitcast.108), channel_id=1, replica_groups=mesh['zlo'=2,'x'=4,'core'=2,'zhi'=4,'yhi'=4,'ylo'=2] {'zlo','x','core'}, dimensions={0} | all-to-all | bytes 524288 | tf_op jit(solution)/shard_map/all_to_all | solution.py:16
  130.1 21.3 %all_to_all.32 = f32[32,16,256]{2,1,0:T(8,128)S(1)} all-to-all(f32[32,16,256]{2,1,0:T(8,128)S(1)} %broadcast_in_dim.95), channel_id=1, replica_groups=mesh['zlo'=2,'x'=4,'core'=2,'zhi'=4,'yhi'=4,'ylo'=2] {'zhi','yhi','ylo'}, dimensions={0} | all-to-all | bytes 1048576 | tf_op jit(solution)/shard_map/all_to_all | solution.py:16
  151.4 5.7 %collective-permute-start.1 = (f32[32,16,256]{2,1,0:T(8,128)S(1)}, f32[32,16,256]{2,1,0:T(8,128)S(1)}, u32[]{:S(2)}, u32[]{:S(2)}) collective-permute-start(f32[32,16,256]{2,1,0:T(8,128)S(1)} %all_to_all.32), channel_id=1, source_target_pairs={{0,32},{32,0},{1,33},{33,1},{2,34},{34,2},{3,35},{35,3},{4,36},{36... | collective-permute-start | bytes 1572872 | tf_op jit(solution)/shard_map/ppermute | solution.py:99
  157.1 0.6 copy.36
  157.8 0.1 dynamic-slice_bitcast_fusion
  157.9 0.7 copy.34
  158.8 1.1 copy-done.1
  160.0 1.1 bitcast_subtract_fusion
  (29 shorter events, 1.0 us)
Async XLA Ops:
  0.6 44.1 %copy-start = (f32[512,256]{1,0:T(8,128)S(1)}, f32[512,256]{1,0:T(8,128)}, u32[]{:S(2)}) copy-start(f32[512,256]{1,0:T(8,128)} %param.5) | copy-start | bytes 1572868
  0.6 14.3 %collective-permute-start = (f32[32,512]{1,0:T(8,128)}, f32[32,512]{1,0:T(8,128)S(1)}, u32[]{:S(2)}, u32[]{:S(2)}) collective-permute-start(f32[32,512]{1,0:T(8,128)} %bitcast.113), channel_id=1, source_target_pairs={{0,0},{1,64},{2,128},{3,192},{4,256},{5,320},{6,384},{7,448},{8,1}... | collective-permute-start | bytes 196616 | tf_op jit(solution)/shard_map/ppermute | solution.py:41
  6.4 0.7 copy-start.4
  6.4 0.8 copy-start.3
  15.6 7.5 %all-to-all-start = ((f32[4,16,256]{2,1,0:T(8,128)}), f32[4,16,256]{2,1,0:T(8,128)S(1)}, u32[]{:S(2)}, u32[]{:S(2)}) async-start(f32[4,16,256]{2,1,0:T(8,128)} %bitcast.9), calls=%async_computation | async-start | bytes 131072 | tf_op jit(solution)/shard_map/all_to_all | solution.py:16
  24.0 20.5 %all-to-all-start.1 = ((f32[16,32,256]{2,1,0:T(8,128)}), f32[16,32,256]{2,1,0:T(8,128)S(1)}, u32[]{:S(2)}, u32[]{:S(2)}) async-start(f32[16,32,256]{2,1,0:T(8,128)} %broadcast_in_dim.89), calls=%async_computation.1 | async-start | bytes 1048576 | tf_op jit(solution)/shard_map/all_to_all | solution.py:16
  46.3 41.0 %all-to-all-start.2 = ((f32[32,16,512]{2,1,0:T(8,128)}), f32[32,16,512]{2,1,0:T(8,128)S(1)}, u32[]{:S(2)}, u32[]{:S(2)}) async-start(f32[32,16,512]{2,1,0:T(8,128)} %bitcast.28), calls=%async_computation.2 | async-start | bytes 2097152 | tf_op jit(solution)/shard_map/all_to_all | solution.py:16
  87.6 24.9 %copy-start.2 = (f32[512,32]{0,1:T(8,128)S(1)}, f32[512,32]{0,1:T(8,128)}, u32[]{:S(2)}) copy-start(f32[512,32]{0,1:T(8,128)} %param.6) | copy-start | bytes 196612
  151.4 7.3 %collective-permute-start.1 = (f32[32,16,256]{2,1,0:T(8,128)S(1)}, f32[32,16,256]{2,1,0:T(8,128)S(1)}, u32[]{:S(2)}, u32[]{:S(2)}) collective-permute-start(f32[32,16,256]{2,1,0:T(8,128)S(1)} %all_to_all.32), channel_id=1, source_target_pairs={{0,32},{32,0},{1,33},{33,1},{2,34},{34,2},{3,35},{35,3},{4,36},{36... | collective-permute-start | bytes 1572872 | tf_op jit(solution)/shard_map/ppermute | solution.py:99
  158.8 1.2 copy-start.1

commit v4 on v2

--- a/solution.py
+++ b/solution.py
@@ -48,18 +48,23 @@
     sibling = jnp.arange(SIBS, dtype=jnp.int32)[None, :]
     first = jnp.min(jnp.where(named, sibling, SIBS), axis=1)
     last = jnp.max(jnp.where(named, sibling, -1), axis=1)
+    slots = jnp.stack([first, last], axis=1)
+    chosen = (slots[0][:, None] == sibling).reshape(8)
+    matched = (slots[1:3].reshape(4)[:, None] == slots[0][None, :]).reshape(8)
+    placed = (slots[3][:, None] == sibling).reshape(8)
+    masks = jnp.concatenate([chosen, matched, placed]).astype(jnp.float32)
+    masks = lax.optimization_barrier(jnp.broadcast_to(masks[:, None], (24, NB)))
+    chosen = masks[0:8].reshape(2, SIBS, 1, NB)
+    matched = masks[8:16].reshape(2, 2, 2, 1, 1, NB)
+    placed = masks[16:24].reshape(2, SIBS, 1, NB)
 
-    halves = moved.reshape(32, 2, NB).transpose(1, 0, 2)
-    whole = exchange(to_all(halves, NROW).reshape(NCOL, 32, NB), PROW + ("ylo",))
-    whole = whole.reshape(8, SIBS, 32, NB)
+    parts = moved.reshape(2, 16, 2, NB).transpose(0, 2, 1, 3).reshape(SIBS, 16, NB)
+    parts = exchange(parts, ("core", "ylo"))
+    parts = jnp.sum(chosen * parts[None], axis=1)
+    block = exchange(to_all(parts.reshape(32, NB), NROW), PROW).reshape(NROW, 2, 16, NB)
 
-    sides = []
-    for h in range(2):
-        for want in (first[1 + h], last[1 + h]):
-            side = lax.dynamic_index_in_dim(whole, want, 1)
-            held = (first[0] == want) | (last[0] == want)
-            sides.append(jnp.where(held, side, 0.0))
-    sides = jnp.stack(sides).reshape(2, 512, NB)
+    sides = matched[:, :, 0] * block[None, None, :, 0] + matched[:, :, 1] * block[None, None, :, 1]
+    sides = sides.reshape(2, 512, NB)
     product = lax.dot_general(
         trailing.reshape(2, NB, NB),
         sides,
@@ -70,14 +75,7 @@
     pieces = exchange(product.reshape(NCOL, 16, 512), PCOL)
     reduced = jnp.sum(pieces, axis=0).reshape(16, 2, NB)
 
-    result = jnp.stack(
-        [
-            jnp.where(
-                first[3] == s, -reduced[:, 0], jnp.where(last[3] == s, -reduced[:, 1], 0.0)
-            )
-            for s in range(SIBS)
-        ]
-    )
+    result = -(placed[0] * reduced[None, :, 0] + placed[1] * reduced[None, :, 1])
     inv_panel = result.transpose(1, 0, 2).reshape(16, SIBS * NB)
 
     upper = jnp.broadcast_to(result[:, None], (SIBS, 8, 16, NB)).reshape(NCOL, 16, NB)

time: 164 us -> 160 us (0.976)
  between operations: 23.6 us -> 1.01 us
  waiting for transfers between devices: 30.5 us -> 47.1 us
  starting transfers between devices: 35.8 us -> 40 us
  blocking collectives: 63.4 us -> 60.7 us
    all_to_all x2 -> x3, waiting for transfers between devices: 21.9 us -> 40.8 us  [exchange(): return lax.all_to_all(array, axes, 0, 0, tiled=True)]
    all_to_all x2 -> x3, starting transfers between devices: 24.4 us -> 28.5 us  [exchange(): return lax.all_to_all(array, axes, 0, 0, tiled=True)]
    all_to_all x3, blocking collectives: 63.4 us -> 60.7 us  [exchange(): return lax.all_to_all(array, axes, 0, 0, tiled=True)]
    ppermute x1, waiting for transfers between devices: 8.56 us -> 6.31 us  [shards(): moved = lax.ppermute(factor_t, PROW + PCOL, column_of_block())]
  transfers between devices with their start and end apart: 4 -> 5, of which waited for: 2 -> 4; matrix products, arithmetic and copies ran while one was open for 2% -> 2% of each run, Pallas kernels for 0% -> 0%
where the time goes in v4:
time: 160 us; the launch traced here: 159 us
  blocking collectives  60.7 us (38%)
  waiting for transfers between devices  47.1 us (29%)
  starting transfers between devices  40 us (25%)
  local copies, waits for them, and re-layouts  5.29 us (3%)
  other arithmetic  3.03 us (2%)
  matrix products  1.84 us (1%)
    all_to_all x3, blocking collectives, exchange(): return lax.all_to_all(array, axes, 0, 0, tiled=True)  60.7 us
    all_to_all x3, waiting for transfers between devices, exchange(): return lax.all_to_all(array, axes, 0, 0, tiled=True)  40.8 us
    all_to_all x3, starting transfers between devices, exchange(): return lax.all_to_all(array, axes, 0, 0, tiled=True)  28.5 us
    ppermute x1, waiting for transfers between devices, shards(): moved = lax.ppermute(factor_t, PROW + PCOL, column_of_block())  6.31 us
    ppermute x1, starting transfers between devices, shards(): moved = lax.ppermute(factor_t, PROW + PCOL, column_of_block())  5.73 us
    ppermute x1, starting transfers between devices, shards(): other = lax.ppermute(mine, 'core', [(0, 1), (1, 0)])  5.7 us
  transfers between devices with their start and end apart: 5, of which 4 were waited for; matrix products, arithmetic and copies ran while one was open for 2% of the time, Pallas kernels for 0%

profile of v4, /device:TPU:1, one launch (start us, length us, event | category | flops | bytes accessed | tf_op | source)
XLA Modules:
  0.0 158.9 jit_solution(16794824227918255156)
XLA Ops:
  0.6 5.7 %collective-permute-start = (f32[32,512]{1,0:T(8,128)}, f32[32,512]{1,0:T(8,128)S(1)}, u32[]{:S(2)}, u32[]{:S(2)}) collective-permute-start(f32[32,512]{1,0:T(8,128)} %bitcast.88), channel_id=1, source_target_pairs={{0,0},{1,64},{2,128},{3,192},{4,256},{5,320},{6,384},{7,448},{8,1}... | collective-permute-start | bytes 196616 | tf_op jit(solution)/shard_map/ppermute | solution.py:41
  6.5 0.6 copy-done.4
  7.1 0.2 select_reduce_fusion.2
  7.3 0.2 compare_reduce_fusion
  7.7 0.2 slice_reduce_fusion.1
  8.6 6.3 %collective-permute-done = f32[32,512]{1,0:T(8,128)S(1)} collective-permute-done((f32[32,512]{1,0:T(8,128)}, f32[32,512]{1,0:T(8,128)S(1)}, u32[]{:S(2)}, u32[]{:S(2)}) %collective-permute-start) | collective-permute-done | bytes 65568 | tf_op jit(solution)/shard_map/ppermute | solution.py:41
  15.0 0.6 copy.18
  15.6 3.3 %all-to-all-start = ((f32[4,16,256]{2,1,0:T(8,128)}), f32[4,16,256]{2,1,0:T(8,128)S(1)}, u32[]{:S(2)}, u32[]{:S(2)}) async-start(f32[4,16,256]{2,1,0:T(8,128)} %bitcast.9), calls=%async_computation | async-start | bytes 131072 | tf_op jit(solution)/shard_map/all_to_all | solution.py:16
  18.9 2.9 %all-to-all-done = f32[4,16,256]{2,1,0:T(8,128)S(1)} async-done(((f32[4,16,256]{2,1,0:T(8,128)}), f32[4,16,256]{2,1,0:T(8,128)S(1)}, u32[]{:S(2)}, u32[]{:S(2)}) %all-to-all-start) | async-done | bytes 65568 | tf_op jit(solution)/shard_map/all_to_all | solution.py:16
  21.9 0.8 broadcast_in_dim.79
  22.7 11.8 %all-to-all-start.1 = ((f32[16,32,256]{2,1,0:T(8,128)}), f32[16,32,256]{2,1,0:T(8,128)S(1)}, u32[]{:S(2)}, u32[]{:S(2)}) async-start(f32[16,32,256]{2,1,0:T(8,128)} %broadcast_in_dim.79), calls=%async_computation.1 | async-start | bytes 1048576 | tf_op jit(solution)/shard_map/all_to_all | solution.py:16
  34.6 9.6 %all-to-all-done.1 = f32[16,32,256]{2,1,0:T(8,128)S(1)} async-done(((f32[16,32,256]{2,1,0:T(8,128)}), f32[16,32,256]{2,1,0:T(8,128)S(1)}, u32[]{:S(2)}, u32[]{:S(2)}) %all-to-all-start.1) | async-done | bytes 524320 | tf_op jit(solution)/shard_map/all_to_all | solution.py:16
  44.5 1.6 fusion.5
  46.1 13.4 %all-to-all-start.2 = ((f32[32,16,512]{2,1,0:T(8,128)}), f32[32,16,512]{2,1,0:T(8,128)S(1)}, u32[]{:S(2)}, u32[]{:S(2)}) async-start(f32[32,16,512]{2,1,0:T(8,128)} %bitcast.19), calls=%async_computation.2 | async-start | bytes 2097152 | tf_op jit(solution)/shard_map/all_to_all | solution.py:16
  59.5 28.2 %all-to-all-done.2 = f32[32,16,512]{2,1,0:T(8,128)S(1)} async-done(((f32[32,16,512]{2,1,0:T(8,128)}), f32[32,16,512]{2,1,0:T(8,128)S(1)}, u32[]{:S(2)}, u32[]{:S(2)}) %all-to-all-start.2) | async-done | bytes 1048608 | tf_op jit(solution)/shard_map/all_to_all | solution.py:16
  88.0 22.6 %all_to_all.30 = f32[32,16,256]{2,1,0:T(8,128)S(1)} all-to-all(f32[32,16,256]{2,1,0:T(8,128)S(1)} %bitcast.73), channel_id=1, replica_groups=mesh['zlo'=2,'x'=4,'core'=2,'zhi'=4,'yhi'=4,'ylo'=2] {'zhi','yhi','ylo'}, dimensions={0} | all-to-all | bytes 1048576 | tf_op jit(solution)/shard_map/all_to_all | solution.py:16
  110.6 0.3 fusion.6
  110.9 16.7 %all_to_all.31 = f32[16,16,256]{2,1,0:T(8,128)S(1)} all-to-all(f32[16,16,256]{2,1,0:T(8,128)S(1)} %bitcast.76), channel_id=1, replica_groups=mesh['zlo'=2,'x'=4,'core'=2,'zhi'=4,'yhi'=4,'ylo'=2] {'zlo','x','core'}, dimensions={0} | all-to-all | bytes 524288 | tf_op jit(solution)/shard_map/all_to_all | solution.py:16
  127.7 21.3 %all_to_all.32 = f32[32,16,256]{2,1,0:T(8,128)S(1)} all-to-all(f32[32,16,256]{2,1,0:T(8,128)S(1)} %broadcast_in_dim.83), channel_id=1, replica_groups=mesh['zlo'=2,'x'=4,'core'=2,'zhi'=4,'yhi'=4,'ylo'=2] {'zhi','yhi','ylo'}, dimensions={0} | all-to-all | bytes 1048576 | tf_op jit(solution)/shard_map/all_to_all | solution.py:16
  149.0 5.7 %collective-permute-start.1 = (f32[32,16,256]{2,1,0:T(8,128)S(1)}, f32[32,16,256]{2,1,0:T(8,128)S(1)}, u32[]{:S(2)}, u32[]{:S(2)}) collective-permute-start(f32[32,16,256]{2,1,0:T(8,128)S(1)} %all_to_all.32), channel_id=1, source_target_pairs={{0,32},{32,0},{1,33},{33,1},{2,34},{34,2},{3,35},{35,3},{4,36},{36... | collective-permute-start | bytes 1572872 | tf_op jit(solution)/shard_map/ppermute | solution.py:90
  154.9 0.6 add_negate_fusion.1
  155.7 0.7 copy.19
  156.6 1.1 copy-done.1
  157.8 1.1 bitcast_subtract_fusion
  (54 shorter events, 2.1 us)
Async XLA Ops:
  0.6 43.8 %copy-start = (f32[512,256]{1,0:T(8,128)S(1)}, f32[512,256]{1,0:T(8,128)}, u32[]{:S(2)}) copy-start(f32[512,256]{1,0:T(8,128)} %param.5) | copy-start | bytes 1572868
  0.6 14.3 %collective-permute-start = (f32[32,512]{1,0:T(8,128)}, f32[32,512]{1,0:T(8,128)S(1)}, u32[]{:S(2)}, u32[]{:S(2)}) collective-permute-start(f32[32,512]{1,0:T(8,128)} %bitcast.88), channel_id=1, source_target_pairs={{0,0},{1,64},{2,128},{3,192},{4,256},{5,320},{6,384},{7,448},{8,1}... | collective-permute-start | bytes 196616 | tf_op jit(solution)/shard_map/ppermute | solution.py:41
  6.4 0.7 copy-start.4
  6.4 0.8 copy-start.3
  15.6 6.2 %all-to-all-start = ((f32[4,16,256]{2,1,0:T(8,128)}), f32[4,16,256]{2,1,0:T(8,128)S(1)}, u32[]{:S(2)}, u32[]{:S(2)}) async-start(f32[4,16,256]{2,1,0:T(8,128)} %bitcast.9), calls=%async_computation | async-start | bytes 131072 | tf_op jit(solution)/shard_map/all_to_all | solution.py:16
  22.7 21.5 %all-to-all-start.1 = ((f32[16,32,256]{2,1,0:T(8,128)}), f32[16,32,256]{2,1,0:T(8,128)S(1)}, u32[]{:S(2)}, u32[]{:S(2)}) async-start(f32[16,32,256]{2,1,0:T(8,128)} %broadcast_in_dim.79), calls=%async_computation.1 | async-start | bytes 1048576 | tf_op jit(solution)/shard_map/all_to_all | solution.py:16
  46.1 41.7 %all-to-all-start.2 = ((f32[32,16,512]{2,1,0:T(8,128)}), f32[32,16,512]{2,1,0:T(8,128)S(1)}, u32[]{:S(2)}, u32[]{:S(2)}) async-start(f32[32,16,512]{2,1,0:T(8,128)} %bitcast.19), calls=%async_computation.2 | async-start | bytes 2097152 | tf_op jit(solution)/shard_map/all_to_all | solution.py:16
  88.0 22.6 %copy-start.2 = (f32[512,32]{0,1:T(8,128)S(1)}, f32[512,32]{0,1:T(8,128)}, u32[]{:S(2)}) copy-start(f32[512,32]{0,1:T(8,128)} %param.6) | copy-start | bytes 196612
  149.0 7.4 %collective-permute-start.1 = (f32[32,16,256]{2,1,0:T(8,128)S(1)}, f32[32,16,256]{2,1,0:T(8,128)S(1)}, u32[]{:S(2)}, u32[]{:S(2)}) collective-permute-start(f32[32,16,256]{2,1,0:T(8,128)S(1)} %all_to_all.32), channel_id=1, source_target_pairs={{0,32},{32,0},{1,33},{33,1},{2,34},{34,2},{3,35},{35,3},{4,36},{36... | collective-permute-start | bytes 1572872 | tf_op jit(solution)/shard_map/ppermute | solution.py:90
  156.5 1.2 copy-start.1

commit v5 on v4

--- a/solution.py
+++ b/solution.py
@@ -1,6 +1,8 @@
 import jax
 import jax.numpy as jnp
 from jax import lax
+from jax.experimental import pallas as pl
+from jax.experimental.pallas import tpu as pltpu
 from jax.sharding import Mesh, PartitionSpec as P
 
 NB = 256
@@ -9,6 +11,7 @@
 PCOL = ("zhi", "yhi", "ylo")
 NROW = 16
 NCOL = 32
+LANES = 128
 HIGH = lax.Precision.HIGH
 
 
@@ -31,14 +34,49 @@
     return pairs
 
 
+def assemble_kernel(core_ref, mine_ref, other_ref, diag_ref, out_ref):
+    low_is_mine = core_ref[0] == 0
+    for half in range(2):
+        lanes = pl.ds(half * LANES, LANES)
+        for part in range(4):
+            for e in range(2):
+                mine = mine_ref[half * 4 + part, pl.ds(e * 16, 16), :]
+                other = other_ref[half * 4 + part, pl.ds(e * 16, 16), :]
+                low = jnp.where(low_is_mine, mine, other)
+                high = jnp.where(low_is_mine, other, mine)
+                first = (e * 4 + part) * 32
+                for rows, term in ((pl.ds(first, 16), low), (pl.ds(first + 16, 16), high)):
+                    out_ref[0, rows, lanes] = diag_ref[0, rows, lanes] - term
+
+
+def assemble(core, mine, other, diag_inv):
+    pieces = pl.BlockSpec((8, 32, LANES), lambda s, core_ref: (s, 0, 0))
+    block = pl.BlockSpec((1, NB, NB), lambda s, core_ref: (s, 0, 0))
+    return pl.pallas_call(
+        assemble_kernel,
+        grid_spec=pltpu.PrefetchScalarGridSpec(
+            num_scalar_prefetch=1,
+            grid=(SIBS,),
+            in_specs=[pieces, pieces, block],
+            out_specs=block,
+        ),
+        out_shape=jax.ShapeDtypeStruct((SIBS, NB, NB), jnp.float32),
+        compiler_params=pltpu.CompilerParams(vmem_limit_bytes=4 * 1024 * 1024),
+    )(core, mine, other, diag_inv)
+
+
 def shards(trailing, panels, diag_inv, ancestors, owner_map):
     row = lax.axis_index(PROW)
     col = lax.axis_index(PCOL)
-    core = lax.axis_index("core")
     nblk = owner_map.shape[0]
 
     factor_t = panels.T
     moved = lax.ppermute(factor_t, PROW + PCOL, column_of_block())
+    across = lax.ppermute(factor_t, "yhi", [(0, 2), (1, 3), (2, 0), (3, 1)])
+    right = lax.axis_index("yhi") >= 2
+    pair = jnp.concatenate(
+        [jnp.where(right, across, factor_t), jnp.where(right, factor_t, across)]
+    )
 
     blocks = jnp.stack([col, 2 * row, 2 * row + 1, 2 * row + col // 16])
     number = jnp.sum(
@@ -78,20 +116,18 @@
     result = -(placed[0] * reduced[None, :, 0] + placed[1] * reduced[None, :, 1])
     inv_panel = result.transpose(1, 0, 2).reshape(16, SIBS * NB)
 
-    upper = jnp.broadcast_to(result[:, None], (SIBS, 8, 16, NB)).reshape(NCOL, 16, NB)
-    upper = exchange(upper, PCOL).reshape(512, NB)
-    part = lax.dynamic_slice_in_dim(upper, col % 8 * 32, 32, 1)
-    inv_upper = part.T
+    upper = result.reshape(SIBS, 16, 2, LANES).transpose(0, 2, 1, 3)
+    upper = jnp.broadcast_to(upper[:, :, None], (SIBS, 2, 4, 16, LANES))
+    upper = exchange(upper.reshape(NCOL, 16, LANES), PCOL).reshape(512, LANES)
+    inv_upper = lax.dynamic_slice_in_dim(upper, col % 4 * 32, 32, 1).T
 
-    term = jnp.dot(factor_t, upper, precision=HIGH, preferred_element_type=jnp.float32)
-    term = exchange(to_all(term.reshape(2, 16, NB), 8).reshape(NROW, 16, NB), PROW)
+    term = jnp.dot(pair, upper, precision=HIGH, preferred_element_type=jnp.float32)
+    term = term.reshape(2, 2, 16, LANES).transpose(1, 0, 2, 3).reshape(2, 32, LANES)
+    term = exchange(to_all(term, 8).reshape(NROW, 32, LANES), PROW)
     term = jnp.sum(term, axis=0)
     mine = exchange(to_all(term, NCOL), PCOL)
     other = lax.ppermute(mine, "core", [(0, 1), (1, 0)])
-    low = jnp.where(core == 0, mine, other).reshape(SIBS, 8, 1, 16, NB)
-    high = jnp.where(core == 0, other, mine).reshape(SIBS, 8, 1, 16, NB)
-    term = jnp.concatenate([low, high], axis=2).reshape(SIBS, NB, NB)
-    inv_diag = diag_inv - term
+    inv_diag = assemble(lax.axis_index("core").reshape(1), mine, other, diag_inv)
     return (inv_panel, inv_upper, inv_diag)
 
 

time: 160 us -> 159 us (level)
  blocking collectives: 60.7 us -> 39.9 us
  starting transfers between devices: 40 us -> 54.6 us
  waiting for transfers between devices: 47.1 us -> 52.2 us
    all_to_all x3 -> x2, blocking collectives: 60.7 us -> 39.9 us  [exchange(): return lax.all_to_all(array, axes, 0, 0, tiled=True)]
    all_to_all x3 -> x4, starting transfers between devices: 28.5 us -> 36 us  [exchange(): return lax.all_to_all(array, axes, 0, 0, tiled=True)]
    ppermute x0 -> x1, starting transfers between devices: none -> 7.05 us  [shards(): across = lax.ppermute(factor_t, 'yhi', [(0, 2), (1, 3), (2, 0), (3, 1)])]
    ppermute x0 -> x1, waiting for transfers between devices: none -> 4.93 us  [shards(): across = lax.ppermute(factor_t, 'yhi', [(0, 2), (1, 3), (2, 0), (3, 1)])]
    all_to_all x3 -> x4, waiting for transfers between devices: 40.8 us -> 41 us  [exchange(): return lax.all_to_all(array, axes, 0, 0, tiled=True)]
  transfers between devices with their start and end apart: 5 -> 7, of which waited for: 4 -> 6; matrix products, arithmetic and copies ran while one was open for 2% -> 2% of each run, Pallas kernels for 0% -> 0%
where the time goes in v5:
time: 159 us; the launch traced here: 158 us
  starting transfers between devices  54.6 us (34%)
  waiting for transfers between devices  52.2 us (33%)
  blocking collectives  39.9 us (25%)
  local copies, waits for them, and re-layouts  4.86 us (3%)
  matrix products  1.8 us (1%)
  other arithmetic  1.77 us (1%)
    all_to_all x4, waiting for transfers between devices, exchange(): return lax.all_to_all(array, axes, 0, 0, tiled=True)  41 us
    all_to_all x2, blocking collectives, exchange(): return lax.all_to_all(array, axes, 0, 0, tiled=True)  39.9 us
    all_to_all x4, starting transfers between devices, exchange(): return lax.all_to_all(array, axes, 0, 0, tiled=True)  36 us
    ppermute x1, starting transfers between devices, shards(): across = lax.ppermute(factor_t, 'yhi', [(0, 2), (1, 3), (2, 0), (3, 1)])  7.05 us
    ppermute x1, waiting for transfers between devices, shards(): moved = lax.ppermute(factor_t, PROW + PCOL, column_of_block())  6.31 us
    ppermute x1, starting transfers between devices, shards(): other = lax.ppermute(mine, 'core', [(0, 1), (1, 0)])  5.83 us
    ppermute x1, starting transfers between devices, shards(): moved = lax.ppermute(factor_t, PROW + PCOL, column_of_block())  5.73 us
    ppermute x1, waiting for transfers between devices, shards(): across = lax.ppermute(factor_t, 'yhi', [(0, 2), (1, 3), (2, 0), (3, 1)])  4.93 us
  transfers between devices with their start and end apart: 7, of which 6 were waited for; matrix products, arithmetic and copies ran while one was open for 2% of the time, Pallas kernels for 0%

profile of v5, /device:TPU:1, one launch (start us, length us, event | category | flops | bytes accessed | tf_op | source)
XLA Modules:
  0.0 157.7 jit_solution(16929918169158979287)
XLA Ops:
  0.6 5.7 %collective-permute-start = (f32[32,512]{1,0:T(8,128)}, f32[32,512]{1,0:T(8,128)S(1)}, u32[]{:S(2)}, u32[]{:S(2)}) collective-permute-start(f32[32,512]{1,0:T(8,128)} %bitcast.96), channel_id=1, source_target_pairs={{0,0},{1,64},{2,128},{3,192},{4,256},{5,320},{6,384},{7,448},{8,1}... | collective-permute-start | bytes 196616 | tf_op jit(solution)/shard_map/ppermute | solution.py:74
  6.5 0.6 copy-done.4
  7.3 0.2 compare_reduce_fusion
  8.6 6.3 %collective-permute-done = f32[32,512]{1,0:T(8,128)S(1)} collective-permute-done((f32[32,512]{1,0:T(8,128)}, f32[32,512]{1,0:T(8,128)S(1)}, u32[]{:S(2)}, u32[]{:S(2)}) %collective-permute-start) | collective-permute-done | bytes 65568 | tf_op jit(solution)/shard_map/ppermute | solution.py:74
  15.0 0.6 copy.24
  15.6 3.3 %all-to-all-start = ((f32[4,16,256]{2,1,0:T(8,128)}), f32[4,16,256]{2,1,0:T(8,128)S(1)}, u32[]{:S(2)}, u32[]{:S(2)}) async-start(f32[4,16,256]{2,1,0:T(8,128)} %bitcast.9), calls=%async_computation | async-start | bytes 131072 | tf_op jit(solution)/shard_map/all_to_all | solution.py:19
  18.9 2.9 %all-to-all-done = f32[4,16,256]{2,1,0:T(8,128)S(1)} async-done(((f32[4,16,256]{2,1,0:T(8,128)}), f32[4,16,256]{2,1,0:T(8,128)S(1)}, u32[]{:S(2)}, u32[]{:S(2)}) %all-to-all-start) | async-done | bytes 65568 | tf_op jit(solution)/shard_map/all_to_all | solution.py:19
  21.9 0.8 broadcast_in_dim.79
  22.7 11.8 %all-to-all-start.1 = ((f32[16,32,256]{2,1,0:T(8,128)}), f32[16,32,256]{2,1,0:T(8,128)S(1)}, u32[]{:S(2)}, u32[]{:S(2)}) async-start(f32[16,32,256]{2,1,0:T(8,128)} %broadcast_in_dim.79), calls=%async_computation.1 | async-start | bytes 1048576 | tf_op jit(solution)/shard_map/all_to_all | solution.py:19
  34.6 9.6 %all-to-all-done.1 = f32[16,32,256]{2,1,0:T(8,128)S(1)} async-done(((f32[16,32,256]{2,1,0:T(8,128)}), f32[16,32,256]{2,1,0:T(8,128)S(1)}, u32[]{:S(2)}, u32[]{:S(2)}) %all-to-all-start.1) | async-done | bytes 524320 | tf_op jit(solution)/shard_map/all_to_all | solution.py:19
  44.5 1.6 %fusion.5 = f32[2,512,256]{1,2,0:T(8,128)} fusion(f32[2,512,256]{2,1,0:T(8,128)S(1)} %fusion, f32[2,256,256]{2,1,0:T(8,128)S(1)} %bitcast.77), kind=kOutput, calls=%fused_computation.35 | convolution fusion | flops 402653184 | bytes 2621440 | tf_op jit(solution)/shard_map/dot_general | solution.py:106
  46.1 13.4 %all-to-all-start.2 = ((f32[32,16,512]{2,1,0:T(8,128)}), f32[32,16,512]{2,1,0:T(8,128)S(1)}, u32[]{:S(2)}, u32[]{:S(2)}) async-start(f32[32,16,512]{2,1,0:T(8,128)} %bitcast.19), calls=%async_computation.2 | async-start | bytes 2097152 | tf_op jit(solution)/shard_map/all_to_all | solution.py:19
  59.5 28.2 %all-to-all-done.2 = f32[32,16,512]{2,1,0:T(8,128)S(1)} async-done(((f32[32,16,512]{2,1,0:T(8,128)}), f32[32,16,512]{2,1,0:T(8,128)S(1)}, u32[]{:S(2)}, u32[]{:S(2)}) %all-to-all-start.2) | async-done | bytes 1048608 | tf_op jit(solution)/shard_map/all_to_all | solution.py:19
  87.9 0.7 broadcast_in_dim.80
  88.7 7.5 %all-to-all-start.3 = ((f32[32,16,128]{2,1,0:T(8,128)}), f32[32,16,128]{2,1,0:T(8,128)S(1)}, u32[]{:S(2)}, u32[]{:S(2)}) async-start(f32[32,16,128]{2,1,0:T(8,128)} %bitcast.24), calls=%async_computation.3 | async-start | bytes 524288 | tf_op jit(solution)/shard_map/all_to_all | solution.py:19
  96.1 7.0 %collective-permute-start.1 = (f32[32,512]{1,0:T(8,128)S(1)}, f32[32,512]{1,0:T(8,128)S(1)}, u32[]{:S(2)}, u32[]{:S(2)}) collective-permute-start(f32[32,512]{1,0:T(8,128)S(1)} %bitcast.97), channel_id=1, source_target_pairs={{0,4},{2,6},{4,0},{6,2},{1,5},{3,7},{5,1},{7,3},{8,12},{10,14},{12... | collective-permute-start | bytes 196616 | tf_op jit(solution)/shard_map/ppermute | solution.py:75
  103.2 4.9 %collective-permute-done.1 = f32[32,512]{1,0:T(8,128)S(1)} collective-permute-done((f32[32,512]{1,0:T(8,128)S(1)}, f32[32,512]{1,0:T(8,128)S(1)}, u32[]{:S(2)}, u32[]{:S(2)}) %collective-permute-start.1) | collective-permute-done | bytes 65568 | tf_op jit(solution)/shard_map/ppermute | solution.py:75
  108.1 0.3 all-to-all-done.3
  108.7 15.9 %all_to_all.30 = f32[16,32,128]{2,1,0:T(8,128)S(1)} all-to-all(f32[16,32,128]{2,1,0:T(8,128)S(1)} %bitcast.83), channel_id=1, replica_groups=mesh['zlo'=2,'x'=4,'core'=2,'zhi'=4,'yhi'=4,'ylo'=2] {'zlo','x','core'}, dimensions={0} | all-to-all | bytes 524288 | tf_op jit(solution)/shard_map/all_to_all | solution.py:19
  124.6 24.0 %all_to_all.31.mine_ref = f32[32,32,128]{2,1,0:T(8,128)S(1)} all-to-all(f32[32,32,128]{2,1,0:T(8,128)S(1)} %broadcast_in_dim.83), channel_id=1, replica_groups=mesh['zlo'=2,'x'=4,'core'=2,'zhi'=4,'yhi'=4,'ylo'=2] {'zhi','yhi','ylo'}, dimensions={0} | all-to-all | bytes 1048576 | tf_op jit(solution)/shard_map/all_to_all | solution.py:19
  148.6 5.8 %collective-permute-start.2 = (f32[32,32,128]{2,1,0:T(8,128)S(1)}, f32[32,32,128]{2,1,0:T(8,128)S(1)}, u32[]{:S(2)}, u32[]{:S(2)}) collective-permute-start(f32[32,32,128]{2,1,0:T(8,128)S(1)} %all_to_all.31.mine_ref), channel_id=1, source_target_pairs={{0,32},{32,0},{1,33},{33,1},{2,34},{34,2},{3,35},{35,3},{4,36},{36... | collective-permute-start | bytes 1572872 | tf_op jit(solution)/shard_map/ppermute | solution.py:129
  154.6 0.6 add_negate_fusion.1
  155.4 0.7 copy.28
  156.1 1.5 shard_map.76
  (62 shorter events, 2.5 us)
Async XLA Ops:
  0.6 43.8 %copy-start = (f32[512,256]{1,0:T(8,128)S(1)}, f32[512,256]{1,0:T(8,128)}, u32[]{:S(2)}) copy-start(f32[512,256]{1,0:T(8,128)} %param.5) | copy-start | bytes 1572868
  0.6 14.3 %collective-permute-start = (f32[32,512]{1,0:T(8,128)}, f32[32,512]{1,0:T(8,128)S(1)}, u32[]{:S(2)}, u32[]{:S(2)}) collective-permute-start(f32[32,512]{1,0:T(8,128)} %bitcast.96), channel_id=1, source_target_pairs={{0,0},{1,64},{2,128},{3,192},{4,256},{5,320},{6,384},{7,448},{8,1}... | collective-permute-start | bytes 196616 | tf_op jit(solution)/shard_map/ppermute | solution.py:74
  6.4 0.7 copy-start.4
  6.4 0.8 copy-start.3
  15.6 6.2 %all-to-all-start = ((f32[4,16,256]{2,1,0:T(8,128)}), f32[4,16,256]{2,1,0:T(8,128)S(1)}, u32[]{:S(2)}, u32[]{:S(2)}) async-start(f32[4,16,256]{2,1,0:T(8,128)} %bitcast.9), calls=%async_computation | async-start | bytes 131072 | tf_op jit(solution)/shard_map/all_to_all | solution.py:19
  22.7 21.5 %all-to-all-start.1 = ((f32[16,32,256]{2,1,0:T(8,128)}), f32[16,32,256]{2,1,0:T(8,128)S(1)}, u32[]{:S(2)}, u32[]{:S(2)}) async-start(f32[16,32,256]{2,1,0:T(8,128)} %broadcast_in_dim.79), calls=%async_computation.1 | async-start | bytes 1048576 | tf_op jit(solution)/shard_map/all_to_all | solution.py:19
  46.1 41.7 %all-to-all-start.2 = ((f32[32,16,512]{2,1,0:T(8,128)}), f32[32,16,512]{2,1,0:T(8,128)S(1)}, u32[]{:S(2)}, u32[]{:S(2)}) async-start(f32[32,16,512]{2,1,0:T(8,128)} %bitcast.19), calls=%async_computation.2 | async-start | bytes 2097152 | tf_op jit(solution)/shard_map/all_to_all | solution.py:19
  88.7 7.5 %copy-start.2 = (f32[512,32]{0,1:T(8,128)S(1)}, f32[512,32]{0,1:T(8,128)}, u32[]{:S(2)}) copy-start(f32[512,32]{0,1:T(8,128)} %param.6) | copy-start | bytes 196612
  88.7 19.7 %all-to-all-start.3 = ((f32[32,16,128]{2,1,0:T(8,128)}), f32[32,16,128]{2,1,0:T(8,128)S(1)}, u32[]{:S(2)}, u32[]{:S(2)}) async-start(f32[32,16,128]{2,1,0:T(8,128)} %bitcast.24), calls=%async_computation.3 | async-start | bytes 524288 | tf_op jit(solution)/shard_map/all_to_all | solution.py:19
  96.1 12.0 %collective-permute-start.1 = (f32[32,512]{1,0:T(8,128)S(1)}, f32[32,512]{1,0:T(8,128)S(1)}, u32[]{:S(2)}, u32[]{:S(2)}) collective-permute-start(f32[32,512]{1,0:T(8,128)S(1)} %bitcast.97), channel_id=1, source_target_pairs={{0,4},{2,6},{4,0},{6,2},{1,5},{3,7},{5,1},{7,3},{8,12},{10,14},{12... | collective-permute-start | bytes 196616 | tf_op jit(solution)/shard_map/ppermute | solution.py:75
  148.6 7.5 %copy-start.1 = (f32[4,256,256]{2,1,0:T(8,128)S(1)}, f32[4,256,256]{2,1,0:T(8,128)}, u32[]{:S(2)}) copy-start(f32[4,256,256]{2,1,0:T(8,128)} %diag_ref.1) | copy-start | bytes 3145732
  148.6 7.5 %collective-permute-start.2 = (f32[32,32,128]{2,1,0:T(8,128)S(1)}, f32[32,32,128]{2,1,0:T(8,128)S(1)}, u32[]{:S(2)}, u32[]{:S(2)}) collective-permute-start(f32[32,32,128]{2,1,0:T(8,128)S(1)} %all_to_all.31.mine_ref), channel_id=1, source_target_pairs={{0,32},{32,0},{1,33},{33,1},{2,34},{34,2},{3,35},{35,3},{4,36},{36... | collective-permute-start | bytes 1572872 | tf_op jit(solution)/shard_map/ppermute | solution.py:129

commit v6 on v5

--- a/solution.py
+++ b/solution.py
@@ -72,12 +72,6 @@
 
     factor_t = panels.T
     moved = lax.ppermute(factor_t, PROW + PCOL, column_of_block())
-    across = lax.ppermute(factor_t, "yhi", [(0, 2), (1, 3), (2, 0), (3, 1)])
-    right = lax.axis_index("yhi") >= 2
-    pair = jnp.concatenate(
-        [jnp.where(right, across, factor_t), jnp.where(right, factor_t, across)]
-    )
-
     blocks = jnp.stack([col, 2 * row, 2 * row + 1, 2 * row + col // 16])
     number = jnp.sum(
         jnp.where(owner_map[None, :] == blocks[:, None], jnp.arange(nblk)[None, :], 0), axis=1
@@ -99,7 +93,15 @@
     parts = moved.reshape(2, 16, 2, NB).transpose(0, 2, 1, 3).reshape(SIBS, 16, NB)
     parts = exchange(parts, ("core", "ylo"))
     parts = jnp.sum(chosen * parts[None], axis=1)
-    block = exchange(to_all(parts.reshape(32, NB), NROW), PROW).reshape(NROW, 2, 16, NB)
+    parts, own = lax.optimization_barrier((parts, factor_t))
+    block = exchange(to_all(parts.reshape(32, NB), NROW), PROW)
+    across = lax.ppermute(own, "yhi", [(0, 2), (1, 3), (2, 0), (3, 1)])
+    right = lax.axis_index("yhi") >= 2
+    pair = jnp.concatenate(
+        [jnp.where(right, across, own), jnp.where(right, own, across)]
+    )
+    block, pair = lax.optimization_barrier((block, pair))
+    block = block.reshape(NROW, 2, 16, NB)
 
     sides = matched[:, :, 0] * block[None, None, :, 0] + matched[:, :, 1] * block[None, None, :, 1]
     sides = sides.reshape(2, 512, NB)

time: 159 us -> 156 us (0.981)
  blocking collectives: 39.9 us -> 57.5 us
  waiting for transfers between devices: 52.2 us -> 40.7 us
  starting transfers between devices: 54.6 us -> 45.9 us
    all_to_all x2 -> x3, blocking collectives: 39.9 us -> 57.5 us  [exchange(): return lax.all_to_all(array, axes, 0, 0, tiled=True)]
    all_to_all x4 -> x3, waiting for transfers between devices: 41 us -> 30.1 us  [exchange(): return lax.all_to_all(array, axes, 0, 0, tiled=True)]
    all_to_all x4 -> x3, starting transfers between devices: 36 us -> 29.3 us  [exchange(): return lax.all_to_all(array, axes, 0, 0, tiled=True)]
    ppermute x1, starting transfers between devices: 7.05 us -> 4.99 us  [shards(): across = lax.ppermute(own, 'yhi', [(0, 2), (1, 3), (2, 0), (3, 1)])]
  transfers between devices with their start and end apart: 7 -> 6, of which waited for: 6 -> 5; matrix products, arithmetic and copies ran while one was open for 2% -> 2% of each run, Pallas kernels for 0% -> 0%
where the time goes in v6:
time: 156 us; the launch traced here: 154 us
  blocking collectives  57.5 us (37%)
  starting transfers between devices  45.9 us (29%)
  waiting for transfers between devices  40.7 us (26%)
  local copies, waits for them, and re-layouts  4.16 us (3%)
  matrix products  1.79 us (1%)
  other arithmetic  1.77 us (1%)
    all_to_all x3, blocking collectives, exchange(): return lax.all_to_all(array, axes, 0, 0, tiled=True)  57.5 us
    all_to_all x3, waiting for transfers between devices, exchange(): return lax.all_to_all(array, axes, 0, 0, tiled=True)  30.1 us
    all_to_all x3, starting transfers between devices, exchange(): return lax.all_to_all(array, axes, 0, 0, tiled=True)  29.3 us
    ppermute x1, waiting for transfers between devices, shards(): moved = lax.ppermute(factor_t, PROW + PCOL, column_of_block())  6.31 us
    ppermute x1, starting transfers between devices, shards(): other = lax.ppermute(mine, 'core', [(0, 1), (1, 0)])  5.83 us
    ppermute x1, starting transfers between devices, shards(): moved = lax.ppermute(factor_t, PROW + PCOL, column_of_block())  5.73 us
    ppermute x1, starting transfers between devices, shards(): across = lax.ppermute(own, 'yhi', [(0, 2), (1, 3), (2, 0), (3, 1)])  4.99 us
    ppermute x1, waiting for transfers between devices, shards(): across = lax.ppermute(own, 'yhi', [(0, 2), (1, 3), (2, 0), (3, 1)])  4.3 us
  transfers between devices with their start and end apart: 6, of which 5 were waited for; matrix products, arithmetic and copies ran while one was open for 2% of the time, Pallas kernels for 0%

profile of v6, /device:TPU:1, one launch (start us, length us, event | category | flops | bytes accessed | tf_op | source)
XLA Modules:
  0.0 154.3 jit_solution(4873368853064451128)
XLA Ops:
  0.6 5.7 %collective-permute-start = (f32[32,512]{1,0:T(8,128)}, f32[32,512]{1,0:T(8,128)S(1)}, u32[]{:S(2)}, u32[]{:S(2)}) collective-permute-start(f32[32,512]{1,0:T(8,128)} %bitcast.95), channel_id=1, source_target_pairs={{0,0},{1,64},{2,128},{3,192},{4,256},{5,320},{6,384},{7,448},{8,1}... | collective-permute-start | bytes 196616 | tf_op jit(solution)/shard_map/ppermute | solution.py:74
  6.5 0.6 copy-done.4
  7.1 0.2 select_reduce_fusion.2
  7.3 0.2 compare_reduce_fusion
  8.6 6.3 %collective-permute-done = f32[32,512]{1,0:T(8,128)S(1)} collective-permute-done((f32[32,512]{1,0:T(8,128)}, f32[32,512]{1,0:T(8,128)S(1)}, u32[]{:S(2)}, u32[]{:S(2)}) %collective-permute-start) | collective-permute-done | bytes 65568 | tf_op jit(solution)/shard_map/ppermute | solution.py:74
  15.0 0.6 copy.24
  15.6 3.3 %all-to-all-start = ((f32[4,16,256]{2,1,0:T(8,128)}), f32[4,16,256]{2,1,0:T(8,128)S(1)}, u32[]{:S(2)}, u32[]{:S(2)}) async-start(f32[4,16,256]{2,1,0:T(8,128)} %bitcast.9), calls=%async_computation | async-start | bytes 131072 | tf_op jit(solution)/shard_map/all_to_all | solution.py:19
  18.9 2.9 %all-to-all-done = f32[4,16,256]{2,1,0:T(8,128)S(1)} async-done(((f32[4,16,256]{2,1,0:T(8,128)}), f32[4,16,256]{2,1,0:T(8,128)S(1)}, u32[]{:S(2)}, u32[]{:S(2)}) %all-to-all-start) | async-done | bytes 65568 | tf_op jit(solution)/shard_map/all_to_all | solution.py:19
  21.9 0.8 broadcast_in_dim.79
  22.7 12.0 %all-to-all-start.1 = ((f32[16,32,256]{2,1,0:T(8,128)}), f32[16,32,256]{2,1,0:T(8,128)S(1)}, u32[]{:S(2)}, u32[]{:S(2)}) async-start(f32[16,32,256]{2,1,0:T(8,128)} %broadcast_in_dim.79), calls=%async_computation.1 | async-start | bytes 1048576 | tf_op jit(solution)/shard_map/all_to_all | solution.py:19
  34.7 5.0 %collective-permute-start.1 = (f32[32,512]{1,0:T(8,128)S(1)}, f32[32,512]{1,0:T(8,128)S(1)}, u32[]{:S(2)}, u32[]{:S(2)}) collective-permute-start(f32[32,512]{1,0:T(8,128)S(1)} %bitcast.96), channel_id=1, source_target_pairs={{0,4},{2,6},{4,0},{6,2},{1,5},{3,7},{5,1},{7,3},{8,12},{10,14},{12... | collective-permute-start | bytes 196616 | tf_op jit(solution)/shard_map/ppermute | solution.py:98
  39.7 4.3 %collective-permute-done.1 = f32[32,512]{1,0:T(8,128)S(1)} collective-permute-done((f32[32,512]{1,0:T(8,128)S(1)}, f32[32,512]{1,0:T(8,128)S(1)}, u32[]{:S(2)}, u32[]{:S(2)}) %collective-permute-start.1) | collective-permute-done | bytes 65568 | tf_op jit(solution)/shard_map/ppermute | solution.py:98
  44.1 0.6 all-to-all-done.1
  44.9 1.6 %fusion.5 = f32[2,512,256]{1,2,0:T(8,128)} fusion(f32[2,512,256]{2,1,0:T(8,128)S(1)} %fusion, f32[2,256,256]{2,1,0:T(8,128)S(1)} %bitcast.75), kind=kOutput, calls=%fused_computation.35 | convolution fusion | flops 402653184 | bytes 2621440 | tf_op jit(solution)/shard_map/dot_general | solution.py:108
  46.5 14.1 %all-to-all-start.2 = ((f32[32,16,512]{2,1,0:T(8,128)}), f32[32,16,512]{2,1,0:T(8,128)S(1)}, u32[]{:S(2)}, u32[]{:S(2)}) async-start(f32[32,16,512]{2,1,0:T(8,128)} %bitcast.19), calls=%async_computation.2 | async-start | bytes 2097152 | tf_op jit(solution)/shard_map/all_to_all | solution.py:19
  60.6 26.6 %all-to-all-done.2 = f32[32,16,512]{2,1,0:T(8,128)S(1)} async-done(((f32[32,16,512]{2,1,0:T(8,128)}), f32[32,16,512]{2,1,0:T(8,128)S(1)}, u32[]{:S(2)}, u32[]{:S(2)}) %all-to-all-start.2) | async-done | bytes 1048608 | tf_op jit(solution)/shard_map/all_to_all | solution.py:19
  87.5 22.1 %all_to_all.30 = f32[32,16,128]{2,1,0:T(8,128)S(1)} all-to-all(f32[32,16,128]{2,1,0:T(8,128)S(1)} %bitcast.81), channel_id=1, replica_groups=mesh['zlo'=2,'x'=4,'core'=2,'zhi'=4,'yhi'=4,'ylo'=2] {'zhi','yhi','ylo'}, dimensions={0} | all-to-all | bytes 524288 | tf_op jit(solution)/shard_map/all_to_all | solution.py:19
  109.6 0.2 convolution_bitcast_fusion
  109.8 15.9 %all_to_all.31 = f32[16,32,128]{2,1,0:T(8,128)S(1)} all-to-all(f32[16,32,128]{2,1,0:T(8,128)S(1)} %bitcast.82), channel_id=1, replica_groups=mesh['zlo'=2,'x'=4,'core'=2,'zhi'=4,'yhi'=4,'ylo'=2] {'zlo','x','core'}, dimensions={0} | all-to-all | bytes 524288 | tf_op jit(solution)/shard_map/all_to_all | solution.py:19
  125.8 19.5 %all_to_all.32.mine_ref = f32[32,32,128]{2,1,0:T(8,128)S(1)} all-to-all(f32[32,32,128]{2,1,0:T(8,128)S(1)} %broadcast_in_dim.83), channel_id=1, replica_groups=mesh['zlo'=2,'x'=4,'core'=2,'zhi'=4,'yhi'=4,'ylo'=2] {'zhi','yhi','ylo'}, dimensions={0} | all-to-all | bytes 1048576 | tf_op jit(solution)/shard_map/all_to_all | solution.py:19
  145.3 5.8 %collective-permute-start.2 = (f32[32,32,128]{2,1,0:T(8,128)S(1)}, f32[32,32,128]{2,1,0:T(8,128)S(1)}, u32[]{:S(2)}, u32[]{:S(2)}) collective-permute-start(f32[32,32,128]{2,1,0:T(8,128)S(1)} %all_to_all.32.mine_ref), channel_id=1, source_target_pairs={{0,32},{32,0},{1,33},{33,1},{2,34},{34,2},{3,35},{35,3},{4,36},{36... | collective-permute-start | bytes 1572872 | tf_op jit(solution)/shard_map/ppermute | solution.py:131
  151.2 0.6 add_negate_fusion.1
  152.0 0.7 copy.28
  152.8 1.5 %shard_map.76 = f32[4,256,256]{2,1,0:T(8,128)} custom-call(s32[1]{0:T(128)} %bitcast.27.core_ref, f32[32,32,128]{2,1,0:T(8,128)S(1)} %all_to_all.32.mine_ref, f32[32,32,128]{2,1,0:T(8,128)S(1)} %collective-permute-done.2.other_ref, f32[4,256,256]{2,1,0:T(8,128)S(1)} %copy-done.1), custom_call_target="tpu_custom_call" | custom-call | tf_op jit(solution)/shard_map/pallas_call | solution.py:55
  (61 shorter events, 2.1 us)
Async XLA Ops:
  0.6 44.3 %copy-start = (f32[512,256]{1,0:T(8,128)S(1)}, f32[512,256]{1,0:T(8,128)}, u32[]{:S(2)}) copy-start(f32[512,256]{1,0:T(8,128)} %param.5) | copy-start | bytes 1572868
  0.6 14.3 %collective-permute-start = (f32[32,512]{1,0:T(8,128)}, f32[32,512]{1,0:T(8,128)S(1)}, u32[]{:S(2)}, u32[]{:S(2)}) collective-permute-start(f32[32,512]{1,0:T(8,128)} %bitcast.95), channel_id=1, source_target_pairs={{0,0},{1,64},{2,128},{3,192},{4,256},{5,320},{6,384},{7,448},{8,1}... | collective-permute-start | bytes 196616 | tf_op jit(solution)/shard_map/ppermute | solution.py:74
  6.4 0.7 copy-start.4
  6.4 0.8 copy-start.3
  15.6 6.2 %all-to-all-start = ((f32[4,16,256]{2,1,0:T(8,128)}), f32[4,16,256]{2,1,0:T(8,128)S(1)}, u32[]{:S(2)}, u32[]{:S(2)}) async-start(f32[4,16,256]{2,1,0:T(8,128)} %bitcast.9), calls=%async_computation | async-start | bytes 131072 | tf_op jit(solution)/shard_map/all_to_all | solution.py:19
  22.7 12.0 %copy-start.2 = (f32[512,32]{0,1:T(8,128)S(1)}, f32[512,32]{0,1:T(8,128)}, u32[]{:S(2)}) copy-start(f32[512,32]{0,1:T(8,128)} %param.6) | copy-start | bytes 196612
  22.7 21.9 %all-to-all-start.1 = ((f32[16,32,256]{2,1,0:T(8,128)}), f32[16,32,256]{2,1,0:T(8,128)S(1)}, u32[]{:S(2)}, u32[]{:S(2)}) async-start(f32[16,32,256]{2,1,0:T(8,128)} %broadcast_in_dim.79), calls=%async_computation.1 | async-start | bytes 1048576 | tf_op jit(solution)/shard_map/all_to_all | solution.py:19
  34.7 9.3 %collective-permute-start.1 = (f32[32,512]{1,0:T(8,128)S(1)}, f32[32,512]{1,0:T(8,128)S(1)}, u32[]{:S(2)}, u32[]{:S(2)}) collective-permute-start(f32[32,512]{1,0:T(8,128)S(1)} %bitcast.96), channel_id=1, source_target_pairs={{0,4},{2,6},{4,0},{6,2},{1,5},{3,7},{5,1},{7,3},{8,12},{10,14},{12... | collective-permute-start | bytes 196616 | tf_op jit(solution)/shard_map/ppermute | solution.py:98
  46.5 40.8 %all-to-all-start.2 = ((f32[32,16,512]{2,1,0:T(8,128)}), f32[32,16,512]{2,1,0:T(8,128)S(1)}, u32[]{:S(2)}, u32[]{:S(2)}) async-start(f32[32,16,512]{2,1,0:T(8,128)} %bitcast.19), calls=%async_computation.2 | async-start | bytes 2097152 | tf_op jit(solution)/shard_map/all_to_all | solution.py:19
  145.3 7.5 %copy-start.1 = (f32[4,256,256]{2,1,0:T(8,128)S(1)}, f32[4,256,256]{2,1,0:T(8,128)}, u32[]{:S(2)}) copy-start(f32[4,256,256]{2,1,0:T(8,128)} %diag_ref.1) | copy-start | bytes 3145732
  145.3 7.5 %collective-permute-start.2 = (f32[32,32,128]{2,1,0:T(8,128)S(1)}, f32[32,32,128]{2,1,0:T(8,128)S(1)}, u32[]{:S(2)}, u32[]{:S(2)}) collective-permute-start(f32[32,32,128]{2,1,0:T(8,128)S(1)} %all_to_all.32.mine_ref), channel_id=1, source_target_pairs={{0,32},{32,0},{1,33},{33,1},{2,34},{34,2},{3,35},{35,3},{4,36},{36... | collective-permute-start | bytes 1572872 | tf_op jit(solution)/shard_map/ppermute | solution.py:131
